TPU v7x, 32 devices: a whole 2x2x4 slice. The times are simulated.
32 devices in a mesh: groups: 2 (over y), tm: 4 (over x, core), rows: 4 (over z).
Axes of the slice: x: 2, y: 2, z: 4, core: 2. Of those that a mesh axis runs over, the one named last changes fastest.
Arguments:
- starts: float32 [8, 256, 4096], P(('groups', 'tm'), 'rows'), parts along dimension 0, may hold values from -1.2 to 1.2
- drive: float32 [256, 4096], P('rows'), may hold values from -0.6 to 0.6
Outputs:
- ends: float32 [8, 256, 4096], P(('groups', 'tm'), 'rows'), parts along dimension 0
There are 2 independent parts, one for each index of `groups`. A program takes and returns all parts, laid end to end along the dimension named above; an argument that names none is the same for every part. Nothing has to cross between parts.
All inputs are finite; a program needn't handle non-finite values.
Results may differ from a plain program's by a relative error of at most 0.00002.
Values sent between devices are 32-bit elements; how exact they have to be, the bound alone decides.
No kernel may reach another device: no remote copies, remote signals or barrier semaphores. Data moves between devices by JAX's collectives and lax.ppermute only.
A program may use at most 64 MiB of HBM per device.

v0:
```python
import functools

import jax
import jax.numpy as jnp
from jax import lax
from jax.experimental import pallas as pl
from jax.experimental.pallas import tpu as pltpu
from jax.sharding import PartitionSpec as P


FINE = 3
WIDE = 8
CUT = 4


diffusion = 2.0
step_fine = 0.1
coarse_step = FINE * step_fine
damping = 1.0 + 4.0 * diffusion * coarse_step

AXES = ("groups", "tm", "rows")


def routed(block, route):
    groups, slices, rows = (lax.axis_size(a) for a in AXES)
    pairs = []
    for g in range(groups):
        for t in range(slices):
            for r in range(rows):
                to_g, to_t, to_r = route(g, t, r)
                source = (g * slices + t) * rows + r
                pairs.append((source, (to_g * slices + to_t) * rows + to_r))
    return lax.ppermute(block, AXES, pairs)


def partner(g, t, r):
    return g, t ^ 1, r


def outward(groups, rows):
    def route(g, t, r):
        to_r = r + 1 if t & 1 else r - 1
        if 0 <= to_r < rows:
            return g, t ^ 1, to_r
        other = g ^ 1
        return (other, t, r) if other < groups else (g, t, r)

    return route


def stage_swap(stage):
    def route(g, t, r):
        chip = t // 2
        if chip == stage:
            return g, t + 2, r
        if chip == stage + 1:
            return g, t - 2, r
        return g, t, r

    return route


def around(v):
    height, width = v.shape
    return (pltpu.roll(v, 1, 0) + pltpu.roll(v, height - 1, 0)) + (
        pltpu.roll(v, 1, 1) + pltpu.roll(v, width - 1, 1)
    )


def fine_of(v, nsum, drive):
    return (
        step_fine * diffusion * nsum
        + v * ((1.0 + step_fine - 4.0 * step_fine * diffusion) - step_fine * (v * v))
        + step_fine * drive
    )


def coarse_of(v, nsum, drive):
    scale = coarse_step / damping
    return (
        scale * diffusion * nsum
        + v * ((1.0 + coarse_step) / damping - scale * (v * v))
        + scale * drive
    )


def compute(kernel, outs, args, **kwargs):
    shapes = [jax.ShapeDtypeStruct(o, jnp.float32) for o in outs]
    vmem = pl.BlockSpec(memory_space=pltpu.VMEM)
    return pl.pallas_call(
        kernel,
        out_shape=shapes,
        in_specs=[vmem] * len(args),
        out_specs=[vmem] * len(outs),
        compiler_params=pltpu.CompilerParams(vmem_limit_bytes=16 << 20),
        **kwargs,
    )(*args)


def same(v):
    return v


def start_of(v, drive, kept=same):
    nsum = around(v)
    coarse = kept(coarse_of(v, nsum, drive))
    fine = kept(fine_of(v, nsum, drive))
    for _ in range(FINE - 1):
        fine = kept(fine_of(fine, around(fine), drive))
    return fine, coarse


def ends_of(first, mine, theirs, drive, kept=same):
    f_a, f_b = picked(first, mine[0], theirs[0])
    g_a, g_b = picked(first, mine[1], theirs[1])
    e_a = g_a + (f_a - g_a)
    e_b = kept(coarse_of(e_a, around(e_a), drive)) + (f_b - g_b)
    return e_a, e_b


def chain(current, d_a, d_b, drive, kept=same):
    e_a = kept(coarse_of(current, around(current), drive)) + d_a
    e_b = kept(coarse_of(e_a, around(e_a), drive)) + d_b
    return e_a, e_b


def picked(first, own, other):
    return jnp.where(first, own, other), jnp.where(first, other, own)


def field(ref, kind, kinds, start, size):
    height = ref.shape[0] // kinds
    return ref.at[pl.ds(pl.multiple_of(kind * height + start, 8), size), :]


def mixed(upper, lower):
    row = lax.broadcasted_iota(jnp.int32, upper.shape, 0)
    return jnp.where(row < CUT, upper, lower)


def sublane(v):
    return lax.broadcasted_iota(jnp.int32, v.shape, 0)


def folded(v):
    width = v.shape[1]
    half, quarter = width // 2, width // 4
    four = mixed(v[:, :half], pltpu.roll(v[:, half:], 4, 0))
    row = sublane(four[:, :quarter])
    two = pltpu.roll(v[:, :quarter], 4, 0)
    for i, shift in ((1, 6), (2, 0), (3, 2)):
        part = v[:, i * quarter : (i + 1) * quarter]
        part = pltpu.roll(part, shift, 0) if shift else part
        two = jnp.where(row < 2 * i, two, part)
    return jnp.concatenate([four, two], axis=1)


def unfolded(v):
    half = v.shape[1] * 2 // 3
    four, two = v[:, :half], v[:, half:]
    low = [pltpu.roll(two, 4, 0), pltpu.roll(two, 2, 0), two, pltpu.roll(two, 6, 0)]
    return mixed(
        jnp.concatenate([four, pltpu.roll(four, 4, 0)], axis=1),
        jnp.concatenate(low, axis=1),
    )


def place():
    t = lax.axis_index("tm")
    return t % 2, t // 2


def at_edge(core):
    r, rows = lax.axis_index("rows"), lax.axis_size("rows")
    return ((core == 0) & (r == 0)) | ((core == 1) & (r == rows - 1))


def inner_row(half, core):
    return pl.multiple_of(8 + (half - 16) * core, 8)


def middle_row(half, core):
    return pl.multiple_of((2 * half - 16) * core, 8)


def outer_row(half, core):
    return pl.multiple_of((2 * half - WIDE) * core, 8)


def load_kernel(half, starts, drive, own, held, inner, sems):
    core, chip = place()
    copies = []
    for i, (row, size) in enumerate(((8, 2 * half - 16), (0, 8), (2 * half - 8, 8))):
        rows = pl.ds(row, size)
        pair = (
            pltpu.make_async_copy(starts.at[0, rows, :], own.at[rows, :], sems.at[2 * i]),
            pltpu.make_async_copy(drive.at[rows, :], held.at[rows, :], sems.at[2 * i + 1]),
        )
        for copy in pair:
            copy.start()
        copies.append(pair)

    for copy in copies[0]:
        copy.wait()

    @pl.when(chip == 0)
    def _():
        rows = pl.ds(inner_row(half, core), half)
        fine, coarse = start_of(own[rows, :], held[rows, :])
        inner[0:half, :] = fine
        inner[half : 2 * half, :] = coarse

    for copy in (*copies[1], *copies[2]):
        copy.wait()


def inner_kernel(half, side, own, other, drive, mine, sent, ends, edge=None):
    core, chip = place()
    first = core == 0
    width = drive.shape[1]
    mid = width // 2

    def columns(ref, rows):
        if side == 0:
            parts = ref[rows, width - 128 :], ref[rows, : mid + 128]
        else:
            parts = ref[rows, mid - 128 :], ref[rows, :128]
        return jnp.concatenate(parts, axis=1)

    @pl.when(chip == 0)
    def _():
        rows = pl.ds(inner_row(half, core), half)
        d = columns(drive, rows)
        theirs = start_of(columns(other, rows), d)
        known = columns(mine, pl.ds(0, half)), columns(mine, pl.ds(half, half))
        e_a, e_b = ends_of(first, known, theirs, d)
        e_a, e_b = e_a[:, 128:-128], e_b[:, 128:-128]
        frame = pltpu.roll(e_b, half - CUT, 0)
        count = half // 8 - 2
        whole = [
            jnp.where(first, frame[8 * i : 8 * i + 8], frame[8 * i + 8 : 8 * i + 16])
            for i in range(count)
        ]
        part = jnp.where(
            first, frame[8 * count : 8 * count + 8], pltpu.roll(frame[:8], 6, 0)
        )
        sent[...] = jnp.concatenate([*whole, folded(part)], axis=1)
        ends[0:half, :] = e_a
        ends[half : 2 * half, :] = e_b

    if edge is not None:
        rows = pl.ds(outer_row(half, core), 8)
        a, b = picked(first, own[rows, :], other[rows, :])
        fields = (jnp.where(first, v, pltpu.roll(v, 6, 0)) for v in (a, b, drive[rows, :]))
        edge[...] = jnp.concatenate([folded(v) for v in fields], axis=1)


def middle_kernel(half, own, other, drive, sent, ends, delta):
    core, chip = place()
    first = core == 0

    @pl.when(chip == 0)
    def _():
        rows = pl.ds(middle_row(half, core), 16)
        d = drive[rows, :]
        mine, theirs = start_of(own[rows, :], d), start_of(other[rows, :], d)
        e_a, e_b = ends_of(first, mine, theirs, d)
        sent[...] = pltpu.roll(e_b, 16 - CUT, 0)[:8]
        ends[0:16, :] = e_a
        ends[16:32, :] = e_b

    @pl.when(chip > 0)
    def _():
        rows = receiver_rows(half, core)
        fine, coarse = start_of(own[rows, :], drive[rows, :])
        delta[...] = fine - coarse


def receiver_rows(half, core):
    return pl.ds(pl.multiple_of((half - WIDE) * core, 8), half + WIDE)


def state_kernel(half, other, drive, theirs):
    core, chip = place()

    @pl.when(chip > 0)
    def _():
        rows = receiver_rows(half, core)
        fine, coarse = start_of(other[rows, :], drive[rows, :])
        theirs[...] = fine - coarse


def outer_window(half, own, other, drive, got):
    core, _ = place()
    first = core == 0
    rows = pl.ds(outer_row(half, core), 8)
    a, b = picked(first, own[rows, :], other[rows, :])
    near = (a, b, drive[rows, :])
    size = got.shape[1] // 3
    far = [unfolded(got[:, i * size : (i + 1) * size]) for i in range(3)]
    far = [jnp.where(first, pltpu.roll(v, 2, 0), v) for v in far]
    upper = [jnp.where(first, f, n) for f, n in zip(far, near)]
    lower = [jnp.where(first, n, f) for f, n in zip(far, near)]
    a, b, d = (jnp.concatenate(p) for p in zip(upper, lower))
    inside = ~(at_edge(core) & (sublane(a) // 8 == core))

    def kept(v):
        return jnp.where(inside, v, 0.0)

    return kept(a), kept(b), d, kept


def outer_kernel(half, own, other, drive, got, mine, theirs, sent, ends, state):
    core, chip = place()
    first = core == 0
    a, b, d, kept = outer_window(half, own, other, drive, got)
    (f_a, g_a), (f_b, g_b) = start_of(a, d, kept), start_of(b, d, kept)

    @pl.when(chip == 0)
    def _():
        e_a = g_a + (f_a - g_a)
        e_b = kept(coarse_of(e_a, around(e_a), d)) + (f_b - g_b)
        frame = pltpu.roll(e_b, 16 - CUT, 0)[:8]
        sent[...] = folded(jnp.where(first, pltpu.roll(frame, 6, 0), frame))
        ends[0:16, :] = e_a
        ends[16:32, :] = e_b

    @pl.when(chip > 0)
    def _():
        rows = pl.ds(pl.multiple_of((half - WIDE) * core, 8), 16)
        before = picked(first, mine[rows, :], theirs[rows, :])
        d_rows = pl.ds(pl.multiple_of((2 * half - 16) * core, 8), 16)
        fields = zip((f_a - g_a, f_b - g_b, d), (*before, drive[d_rows, :]))
        for kind, (v, near) in enumerate(fields):
            top = jnp.where(first, v[:8], near[:8])
            mid = jnp.where(first, mixed(v[8:], near[:8]), mixed(near[8:], v[:8]))
            low = jnp.where(first, near[8:], v[8:])
            state[24 * kind : 24 * kind + 24, :] = jnp.concatenate([top, mid, low])


def inner_end(half, left, right, drive, mine, theirs, keep, send, frame):
    core, chip = place()
    first = core == 0

    @pl.when(chip > 0)
    def _():
        count = half // 8 - 2
        mid = left.shape[1] * 4 // (4 * count + 3)
        parts = left[...], right[...]

        def across(begin, end, change=same):
            return jnp.concatenate([change(p[:, begin:end]) for p in parts], axis=1)

        whole = [across(i * mid, i * mid + mid) for i in range(count)]
        part = across(count * mid, left.shape[1], unfolded)
        upper = [*whole, part]
        lower = [pltpu.roll(part, 2, 0), *whole]
        rows = jnp.concatenate([jnp.where(first, u, v) for u, v in zip(upper, lower)])
        frame[...] = rows
        current = pltpu.roll(jnp.concatenate([rows, rows[:8]]), CUT, 0)
        into = pl.ds(pl.multiple_of(8 * (1 - core), 8), half)
        d_a, d_b = picked(first, mine[into, :], theirs[into, :])
        d = drive[pl.ds(inner_row(half, core), half), :]
        e_a, e_b = chain(current, d_a, d_b, d)
        put_ends(first, e_a[8 : half - 8], e_b[8 : half - 8], keep, send)


def gather_kernel(half, ends_left, ends_right, middle, outer, near_keep, near_send, keep, send):
    core, chip = place()
    first = core == 0
    near = half - 16

    @pl.when(chip == 0)
    def _():
        def rows(kind, begin, size):
            into = pl.ds(half * kind + begin, size)
            return jnp.concatenate([ends_left[into, :], ends_right[into, :]], axis=1)

        def known(kind):
            two = [field(middle, kind, 2, 8 * i, 8)[...] for i in range(2)]
            last = [field(outer, kind, 2, 8 * i, 8)[...] for i in range(2)]
            beside = [rows(kind, 0, 8), rows(kind, half - 8, 8)]
            return jnp.concatenate(
                [
                    rows(kind, 8, near),
                    jnp.where(first, mixed(two[1], beside[0]), mixed(beside[1], two[0])),
                    jnp.where(first, mixed(last[1], two[0]), mixed(two[1], last[0])),
                ]
            )

        put_ends(first, known(0), known(1), keep, send)

    @pl.when(chip > 0)
    def _():
        keep[0:near, :] = near_keep[...]
        send[0:near, :] = near_send[...]


def put_ends(first, e_a, e_b, keep, send):
    kept, sent = picked(first, e_a, e_b)
    keep[...] = kept
    send[...] = sent


def middle_end(half, inner, middle, drive, mine, theirs, keep, send, current):
    core, chip = place()
    first = core == 0
    last = inner.shape[0] - 16

    @pl.when((chip > 0) & first)
    def _():
        current[...] = pltpu.roll(jnp.concatenate([middle[...], inner[0:16, :]]), CUT, 0)

    @pl.when((chip > 0) & (core == 1))
    def _():
        rows = jnp.concatenate([inner[last : last + 16, :], middle[...]])
        current[...] = pltpu.roll(rows, 24 - CUT, 0)

    @pl.when(chip > 0)
    def _():
        rows = pl.ds(pl.multiple_of((half - 16) * core, 8), 24)
        d_a, d_b = picked(first, mine[rows, :], theirs[rows, :])
        d = drive[pl.ds(pl.multiple_of((2 * half - 24) * core, 8), 24), :]
        e_a, e_b = chain(current[...], d_a, d_b, d)
        put_ends(first, e_a[8:16], e_b[8:16], keep, send)


def outer_end(inner, middle, outer, state, keep, send, current):
    core, chip = place()
    first = core == 0
    last = inner.shape[0] - 8

    @pl.when((chip > 0) & first)
    def _():
        part = pltpu.roll(unfolded(outer[...]), 2, 0)
        rows = jnp.concatenate([part, middle[...], inner[0:8, :]])
        current[...] = pltpu.roll(rows, CUT, 0)

    @pl.when((chip > 0) & (core == 1))
    def _():
        rows = jnp.concatenate([inner[last : last + 8, :], middle[...], unfolded(outer[...])])
        current[...] = pltpu.roll(rows, 24 - CUT, 0)

    @pl.when(chip > 0)
    def _():
        d_a, d_b, d = (field(state, kind, 3, 0, 24)[...] for kind in range(3))
        inside = ~(at_edge(core) & (sublane(d) // 8 == 2 * core))
        e_a = coarse_of(current[...], around(current[...]), d) + d_a
        e_a = jnp.where(inside, e_a, 0.0)
        mid = e_a[8:16]
        width = mid.shape[1]
        beside = pltpu.roll(mid, 1, 1) + pltpu.roll(mid, width - 1, 1)
        upright = pltpu.roll(e_a, 1, 0)[8:16] + pltpu.roll(e_a, 23, 0)[8:16]
        e_b = coarse_of(mid, upright + beside, d[8:16]) + d_b[8:16]
        put_ends(first, mid, e_b, keep, send)


def write_kernel(half, last, *refs):
    pieces, out, sems = refs[: 1 if last else 5], refs[-2], refs[-1]
    core, chip = place()

    def copy_all(order):
        copies = []
        for i, (mine, part, source, begin, size) in enumerate(order):
            upper = (16, 8, 0)[part]
            lower = (half, 2 * half - 16, 2 * half - 8)[part]
            row = pl.multiple_of(jnp.where((core == 0) == mine, upper, lower), 8)
            copy = pltpu.make_async_copy(
                pieces[source].at[pl.ds(begin, size), :],
                out.at[0, pl.ds(row, size), :],
                sems.at[i],
            )
            copy.start()
            copies.append(copy)
        for copy in copies:
            copy.wait()

    if last:

        @pl.when(chip > 0)
        def _():
            copy_all(((False, 2, 0, 0, 8),))

    else:
        near = half - 16

        @pl.when(chip == 0)
        def _():
            parts = ((0, 0, near), (1, near, 8), (2, near + 8, 8))
            copy_all(
                [(mine, part, source, *rows) for mine, source in ((True, 0), (False, 1)) for part, *rows in parts]
            )

        @pl.when(chip > 0)
        def _():
            copy_all(
                (
                    (True, 0, 0, 0, near),
                    (False, 0, 1, 0, near),
                    (True, 1, 2, 0, 8),
                    (False, 1, 3, 0, 8),
                    (True, 2, 4, 0, 8),
                )
            )


def written(half, pieces, shape, into=None):
    vmem, anywhere = pl.BlockSpec(memory_space=pltpu.VMEM), pl.BlockSpec(memory_space=pl.ANY)
    extra = () if into is None else (into,)
    return pl.pallas_call(
        functools.partial(write_kernel, half, into is not None),
        out_shape=jax.ShapeDtypeStruct(shape, jnp.float32),
        in_specs=[vmem] * len(pieces) + [anywhere] * len(extra),
        out_specs=anywhere,
        input_output_aliases={len(pieces): 0} if extra else {},
        scratch_shapes=[pltpu.SemaphoreType.DMA((6,))],
        compiler_params=pltpu.CompilerParams(vmem_limit_bytes=16 << 20),
    )(*pieces, *extra)


def after(value, earlier):
    return lax.optimization_barrier((value, earlier))[0]


def masked_update(update, v, drive, inside):
    wide = (
        jnp.roll(v, 1, axis=0) + jnp.roll(v, -1, axis=0)
    ) + (jnp.roll(v, 1, axis=1) + jnp.roll(v, -1, axis=1))
    return jnp.where(inside, update(v, wide, drive), 0.0)


def long_chain(own, drive):
    height = own.shape[0]
    half = height // 2
    groups, slices, rows = (lax.axis_size(a) for a in AXES)
    t, r = lax.axis_index("tm"), lax.axis_index("rows")
    core, chip = t % 2, t // 2
    first = core == 0
    away = outward(groups, rows)

    def cut(field, start, size):
        return lax.dynamic_slice_in_dim(field, start, size, axis=0)

    other = routed(own, partner)
    s_a, s_b = picked(first, own, other)
    edge = core * (height - WIDE)
    got = routed(jnp.concatenate([cut(f, edge, WIDE) for f in (s_a, s_b, drive)]), away)

    def sided(body, outer, inner):
        return jnp.where(
            first,
            jnp.concatenate([outer, body, inner]),
            jnp.concatenate([inner, body, outer]),
        )

    def window(field, place):
        body = cut(field, core * half, half)
        inner = cut(field, jnp.where(first, half, half - WIDE), WIDE)
        return sided(body, got[place * WIDE : (place + 1) * WIDE], inner)

    w_a, w_b, w_d = (window(f, i) for i, f in enumerate((s_a, s_b, drive)))
    row = lax.broadcasted_iota(jnp.int32, (half + 2 * WIDE, 1), 0)
    row = row + r * height + core * half - WIDE
    inside = (row >= 0) & (row < rows * height)
    w_a, w_b = jnp.where(inside, w_a, 0.0), jnp.where(inside, w_b, 0.0)

    def delta(v):
        fine = v
        for _ in range(FINE):
            fine = masked_update(fine_of, fine, w_d, inside)
        return fine - masked_update(coarse_of, v, w_d, inside)

    d_a, d_b = delta(w_a), delta(w_b)

    def both(v):
        e_a = masked_update(coarse_of, v, w_d, inside) + d_a
        return e_a, masked_update(coarse_of, e_a, w_d, inside) + d_b

    def extended(v):
        last = WIDE + half - 2
        inner = routed(cut(v, jnp.where(first, last, WIDE), 2), partner)
        outer = routed(cut(v, jnp.where(first, WIDE, last), 2), away)
        return sided(v[WIDE : WIDE + half], outer, inner)

    e_a, e_b = both(w_a)
    for stage in range(slices // 2 - 1):
        moved = e_b[WIDE - 2 : WIDE + half + 2] if stage == 0 else extended(e_b)
        arrived = routed(moved, stage_swap(stage))
        current = jnp.pad(arrived, ((WIDE - 2, WIDE - 2), (0, 0)))
        n_a, n_b = both(jnp.where(inside, current, 0.0))
        here = chip == stage + 1
        e_a, e_b = jnp.where(here, n_a, e_a), jnp.where(here, n_b, e_b)

    kept, sent = picked(first, e_a[WIDE : WIDE + half], e_b[WIDE : WIDE + half])
    back = routed(sent, partner)
    return jnp.concatenate(picked(first, kept, back))[None]


def on_device(starts, drive):
    own = starts[0]
    if lax.axis_size("tm") != 4:
        return long_chain(own, drive)
    return two_chips(starts, drive)


def two_chips(starts, drive):
    _, height, width = starts.shape
    half = height // 2
    groups, rows = lax.axis_size("groups"), lax.axis_size("rows")
    vmem = pl.BlockSpec(memory_space=pltpu.VMEM)

    other = routed(starts[0], partner)
    own, held, mine = pl.pallas_call(
        functools.partial(load_kernel, half),
        out_shape=[
            jax.ShapeDtypeStruct((size, width), jnp.float32) for size in (height, height, height)
        ],
        in_specs=[pl.BlockSpec(memory_space=pltpu.HBM)] * 2,
        out_specs=[vmem] * 3,
        scratch_shapes=[pltpu.SemaphoreType.DMA((6,))],
        compiler_params=pltpu.CompilerParams(vmem_limit_bytes=50 << 20),
        cost_estimate=pl.CostEstimate(
            flops=60 * 24 * width, bytes_accessed=16 * height * width, transcendentals=0
        ),
        name="load",
    )(starts, drive)
    mid = width // 2
    packed = mid * (half // 8 - 2) + mid * 3 // 4
    sent_l, ends_l = compute(
        functools.partial(inner_kernel, half, 0),
        [(8, packed), (height, mid)],
        (own, other, held, mine),
    )
    here_l = routed(sent_l, stage_swap(0))
    sent_r, ends_r, edge = compute(
        functools.partial(inner_kernel, half, 1),
        [(8, packed), (height, mid), (8, width * 9 // 4)],
        (own, other, held, after(mine, sent_l)),
    )
    here_r = routed(sent_r, stage_swap(0))
    got = routed(edge, outward(groups, rows))
    sent_2, ends_2, delta_own = compute(
        functools.partial(middle_kernel, half),
        [(8, width), (32, width), (half + WIDE, width)],
        (own, other, after(held, sent_r)),
    )
    here_2 = routed(sent_2, stage_swap(0))
    (delta_other,) = compute(
        functools.partial(state_kernel, half), [(half + WIDE, width)], (other, after(held, sent_2))
    )
    sent_3, ends_3, state_3 = compute(
        functools.partial(outer_kernel, half),
        [(8, width * 3 // 4), (32, width), (3 * 24, width)],
        (own, other, held, got, delta_own, delta_other),
    )
    here_3 = routed(sent_3, stage_swap(0))
    near_keep, near_send, frame = compute(
        functools.partial(inner_end, half),
        [(half - 16, width), (half - 16, width), (half - 8, width)],
        (here_l, here_r, held, delta_own, after(delta_other, sent_3)),
    )
    keep_1, send_1 = compute(
        functools.partial(gather_kernel, half),
        [(half, width)] * 2,
        (ends_l, ends_r, ends_2, ends_3, near_keep, near_send),
    )
    back_1 = routed(send_1, partner)
    keep_2, send_2 = compute(
        functools.partial(middle_end, half),
        [(8, width)] * 2,
        (frame, here_2, held, delta_own, after(delta_other, state_3)),
        scratch_shapes=[pltpu.VMEM((24, width), jnp.float32)],
    )
    back_2 = routed(send_2, partner)
    keep_3, send_3 = compute(
        outer_end,
        [(8, width)] * 2,
        (frame, here_2, here_3, after(state_3, keep_2)),
        scratch_shapes=[pltpu.VMEM((24, width), jnp.float32)],
    )
    back_3 = routed(send_3, partner)
    out = written(half, (keep_1, back_1, keep_2, back_2, keep_3), starts.shape)
    return written(half, (back_3,), starts.shape, into=out)


def solution(mesh):
    in_specs = (P(("groups", "tm"), "rows", None), P("rows", None))
    out_specs = P(("groups", "tm"), "rows", None)
    return jax.shard_map(
        on_device, mesh=mesh, in_specs=in_specs, out_specs=out_specs, check_vma=False
    )
```

profile of v0, /device:TPU:0, one launch (start us, length us, event | category | flops | bytes accessed | tf_op | source)
XLA Modules:
  0.0 28.1 jit_solution(492133968332408003)
XLA Ops:
  0.0 0.5 %collective-permute-start = (f32[64,4096]{1,0:T(8,128)}, f32[64,4096]{1,0:T(8,128)S(1)}, u32[]{:S(2)}, u32[]{:S(2)}) collective-permute-start(f32[64,4096]{1,0:T(8,128)} %bitcast.1), channel_id=1, source_target_pairs={{0,4},{1,5},{2,6},{3,7},{4,0},{5,1},{6,2},{7,3},{8,12},{9,13},{10,... | collective-permute-start | bytes 3145736 | tf_op jit(solution)/shard_map/ppermute | solution.py:33
  0.5 2.6 %load.1 = (f32[64,4096]{1,0:T(8,128)S(1)}, f32[64,4096]{1,0:T(8,128)S(1)}, f32[64,4096]{1,0:T(8,128)S(1)}) custom-call(f32[1,64,4096]{2,1,0:T(8,128)} %starts.1, f32[64,4096]{1,0:T(8,128)} %drive.1), custom_call_target="tpu_custom_call" | custom-call | flops 5898240 | bytes 4194304 | tf_op jit(solution)/shard_map/load/pallas_call | solution.py:613
  3.1 0.0 collective-permute-done.other
  3.1 1.0 %shard_map.28 = (f32[8,5632]{1,0:T(8,128)S(1)}, f32[64,2048]{1,0:T(8,128)S(1)}) custom-call(f32[64,4096]{1,0:T(8,128)S(1)} %get-tuple-element.34.own, f32[64,4096]{1,0:T(8,128)S(1)} %collective-permute-done.other, f32[64,4096]{1,0:T(8,128)S(1)} %get-tuple-element.43.drive, f32[64,4096]{1,0:T(8,128)S(1)} %get-tuple-element.38.mine), custom_call_target="tpu_custom_call" | custom-call | tf_op jit(solution)/shard_map/pallas_call | solution.py:90
  4.1 1.1 %shard_map.29 = (f32[8,5632]{1,0:T(8,128)S(1)}, f32[64,2048]{1,0:T(8,128)S(1)}, f32[8,9216]{1,0:T(8,128)S(1)}) custom-call(f32[64,4096]{1,0:T(8,128)S(1)} %get-tuple-element.34.own, f32[64,4096]{1,0:T(8,128)S(1)} %collective-permute-done.other, f32[64,4096]{1,0:T(8,128)S(1)} %get-tuple-element.43.drive, f32[64,4096]{1,0:T(8,128)S(1)} %get-tuple-element.38.mine), custom_call_target="tpu_custom_call" | custom-call | tf_op jit(solution)/shard_map/pallas_call | solution.py:90
  5.2 2.8 %collective-permute-start.3 = (f32[8,9216]{1,0:T(8,128)S(1)}, f32[8,9216]{1,0:T(8,128)S(1)}, u32[]{:S(2)}, u32[]{:S(2)}) collective-permute-start(f32[8,9216]{1,0:T(8,128)S(1)} %get-tuple-element.44), channel_id=1, source_target_pairs={{0,16},{1,4},{2,5},{3,6},{4,1},{5,2},{6,3},{7,23},{8,24},{9,12},{1... | collective-permute-start | bytes 884744 | tf_op jit(solution)/shard_map/ppermute | solution.py:33
  8.0 0.0 collective-permute-start.2
  8.0 2.0 %collective-permute-start.1 = (f32[8,5632]{1,0:T(8,128)S(1)}, f32[8,5632]{1,0:T(8,128)S(1)}, u32[]{:S(2)}, u32[]{:S(2)}) collective-permute-start(f32[8,5632]{1,0:T(8,128)S(1)} %get-tuple-element.37), channel_id=1, source_target_pairs={{0,8},{1,9},{2,10},{3,11},{4,12},{5,13},{6,14},{7,15},{8,0},{9,1},... | collective-permute-start | bytes 540680 | tf_op jit(solution)/shard_map/ppermute | solution.py:33
  10.0 1.4 %shard_map.30 = (f32[8,4096]{1,0:T(8,128)S(1)}, f32[32,4096]{1,0:T(8,128)S(1)}, f32[40,4096]{1,0:T(8,128)S(1)}) custom-call(f32[64,4096]{1,0:T(8,128)S(1)} %get-tuple-element.34.own, f32[64,4096]{1,0:T(8,128)S(1)} %collective-permute-done.other, f32[64,4096]{1,0:T(8,128)S(1)} %get-tuple-element.43.drive), custom_call_target="tpu_custom_call" | custom-call | tf_op jit(solution)/shard_map/pallas_call | solution.py:90
  11.4 1.3 %collective-permute-done.3.got = f32[8,9216]{1,0:T(8,128)S(1)} collective-permute-done((f32[8,9216]{1,0:T(8,128)S(1)}, f32[8,9216]{1,0:T(8,128)S(1)}, u32[]{:S(2)}, u32[]{:S(2)}) %collective-permute-start.3) | collective-permute-done | bytes 294944 | tf_op jit(solution)/shard_map/ppermute | solution.py:33
  12.7 1.5 %shard_map.32 = (f32[8,3072]{1,0:T(8,128)S(1)}, f32[32,4096]{1,0:T(8,128)S(1)}, f32[72,4096]{1,0:T(8,128)S(1)}) custom-call(f32[64,4096]{1,0:T(8,128)S(1)} %get-tuple-element.34.own, f32[64,4096]{1,0:T(8,128)S(1)} %collective-permute-done.other, f32[64,4096]{1,0:T(8,128)S(1)} %get-tuple-element.43.drive, f32[8,9216]{1,0:T(8,128)S(1)} %collective-permute-done.3.got, ...), custom_call_target="tpu_custom_call" | custom-call | tf_op jit(solution)/shard_map/pallas_call | solution.py:90
  14.2 1.2 %collective-permute-done.2.right = f32[8,5632]{1,0:T(8,128)S(1)} collective-permute-done((f32[8,5632]{1,0:T(8,128)S(1)}, f32[8,5632]{1,0:T(8,128)S(1)}, u32[]{:S(2)}, u32[]{:S(2)}) %collective-permute-start.2) | collective-permute-done | bytes 180256 | tf_op jit(solution)/shard_map/ppermute | solution.py:33
  15.4 3.1 %collective-permute-done.1.left = f32[8,5632]{1,0:T(8,128)S(1)} collective-permute-done((f32[8,5632]{1,0:T(8,128)S(1)}, f32[8,5632]{1,0:T(8,128)S(1)}, u32[]{:S(2)}, u32[]{:S(2)}) %collective-permute-start.1) | collective-permute-done | bytes 180256 | tf_op jit(solution)/shard_map/ppermute | solution.py:33
  18.5 0.2 shard_map.36
  18.6 0.1 collective-permute-start.7
  18.7 0.9 %collective-permute-start.4 = (f32[8,4096]{1,0:T(8,128)S(1)}, f32[8,4096]{1,0:T(8,128)S(1)}, u32[]{:S(2)}, u32[]{:S(2)}) collective-permute-start(f32[8,4096]{1,0:T(8,128)S(1)} %get-tuple-element.42), channel_id=1, source_target_pairs={{0,8},{1,9},{2,10},{3,11},{4,12},{5,13},{6,14},{7,15},{8,0},{9,1},... | collective-permute-start | bytes 393224 | tf_op jit(solution)/shard_map/ppermute | solution.py:33
  19.6 1.2 %collective-permute-start.5 = (f32[8,3072]{1,0:T(8,128)S(1)}, f32[8,3072]{1,0:T(8,128)S(1)}, u32[]{:S(2)}, u32[]{:S(2)}) collective-permute-start(f32[8,3072]{1,0:T(8,128)S(1)} %get-tuple-element.45), channel_id=1, source_target_pairs={{0,8},{1,9},{2,10},{3,11},{4,12},{5,13},{6,14},{7,15},{8,0},{9,1},... | collective-permute-start | bytes 294920 | tf_op jit(solution)/shard_map/ppermute | solution.py:33
  20.8 4.3 %collective-permute-done.4.middle = f32[8,4096]{1,0:T(8,128)S(1)} collective-permute-done((f32[8,4096]{1,0:T(8,128)S(1)}, f32[8,4096]{1,0:T(8,128)S(1)}, u32[]{:S(2)}, u32[]{:S(2)}) %collective-permute-start.4) | collective-permute-done | bytes 131104 | tf_op jit(solution)/shard_map/ppermute | solution.py:33
  25.2 0.0 collective-permute-start.8
  25.2 1.6 %collective-permute-done.5.outer = f32[8,3072]{1,0:T(8,128)S(1)} collective-permute-done((f32[8,3072]{1,0:T(8,128)S(1)}, f32[8,3072]{1,0:T(8,128)S(1)}, u32[]{:S(2)}, u32[]{:S(2)}) %collective-permute-start.5) | collective-permute-done | bytes 98336 | tf_op jit(solution)/shard_map/ppermute | solution.py:33
  26.7 0.0 collective-permute-start.6
  26.7 0.0 collective-permute-done.8.refs_3_
  26.7 0.0 collective-permute-done.7.refs_1_
  26.7 1.0 %shard_map.37.refs_1_ = f32[1,64,4096]{2,1,0:T(8,128)} custom-call(f32[32,4096]{1,0:T(8,128)S(1)} %get-tuple-element.59.refs_0_, f32[32,4096]{1,0:T(8,128)S(1)} %collective-permute-done.7.refs_1_, f32[8,4096]{1,0:T(8,128)S(1)} %get-tuple-element.50.refs_2_, f32[8,4096]{1,0:T(8,128)S(1)} %collective-permute-done.8.refs_3_, ...), custom_call_target="tpu_custom_call" | custom-call | tf_op jit(solution)/shard_map/pallas_call | solution.py:510
  27.8 0.3 %collective-permute-done.6.refs_0_ = f32[8,4096]{1,0:T(8,128)S(1)} collective-permute-done((f32[8,4096]{1,0:T(8,128)S(1)}, f32[8,4096]{1,0:T(8,128)S(1)}, u32[]{:S(2)}, u32[]{:S(2)}) %collective-permute-start.6) | collective-permute-done | bytes 131104 | tf_op jit(solution)/shard_map/ppermute | solution.py:33
  28.1 0.1 shard_map.38
  (4 shorter events, 0.0 us)
Async XLA Ops:
  0.0 3.1 %collective-permute-start = (f32[64,4096]{1,0:T(8,128)}, f32[64,4096]{1,0:T(8,128)S(1)}, u32[]{:S(2)}, u32[]{:S(2)}) collective-permute-start(f32[64,4096]{1,0:T(8,128)} %bitcast.1), channel_id=1, source_target_pairs={{0,4},{1,5},{2,6},{3,7},{4,0},{5,1},{6,2},{7,3},{8,12},{9,13},{10,... | collective-permute-start | bytes 3145736 | tf_op jit(solution)/shard_map/ppermute | solution.py:33
  5.2 7.5 %collective-permute-start.3 = (f32[8,9216]{1,0:T(8,128)S(1)}, f32[8,9216]{1,0:T(8,128)S(1)}, u32[]{:S(2)}, u32[]{:S(2)}) collective-permute-start(f32[8,9216]{1,0:T(8,128)S(1)} %get-tuple-element.44), channel_id=1, source_target_pairs={{0,16},{1,4},{2,5},{3,6},{4,1},{5,2},{6,3},{7,23},{8,24},{9,12},{1... | collective-permute-start | bytes 884744 | tf_op jit(solution)/shard_map/ppermute | solution.py:33
  8.0 7.4 %collective-permute-start.2 = (f32[8,5632]{1,0:T(8,128)S(1)}, f32[8,5632]{1,0:T(8,128)S(1)}, u32[]{:S(2)}, u32[]{:S(2)}) collective-permute-start(f32[8,5632]{1,0:T(8,128)S(1)} %get-tuple-element.39), channel_id=1, source_target_pairs={{0,8},{1,9},{2,10},{3,11},{4,12},{5,13},{6,14},{7,15},{8,0},{9,1},... | collective-permute-start | bytes 540680 | tf_op jit(solution)/shard_map/ppermute | solution.py:33
  8.0 10.5 %collective-permute-start.1 = (f32[8,5632]{1,0:T(8,128)S(1)}, f32[8,5632]{1,0:T(8,128)S(1)}, u32[]{:S(2)}, u32[]{:S(2)}) collective-permute-start(f32[8,5632]{1,0:T(8,128)S(1)} %get-tuple-element.37), channel_id=1, source_target_pairs={{0,8},{1,9},{2,10},{3,11},{4,12},{5,13},{6,14},{7,15},{8,0},{9,1},... | collective-permute-start | bytes 540680 | tf_op jit(solution)/shard_map/ppermute | solution.py:33
  18.6 8.1 %collective-permute-start.7 = (f32[32,4096]{1,0:T(8,128)S(1)}, f32[32,4096]{1,0:T(8,128)S(1)}, u32[]{:S(2)}, u32[]{:S(2)}) collective-permute-start(f32[32,4096]{1,0:T(8,128)S(1)} %get-tuple-element.60), channel_id=1, source_target_pairs={{0,4},{1,5},{2,6},{3,7},{4,0},{5,1},{6,2},{7,3},{8,12},{9,13},{10,... | collective-permute-start | bytes 1572872 | tf_op jit(solution)/shard_map/ppermute | solution.py:33
  18.7 6.4 %collective-permute-start.4 = (f32[8,4096]{1,0:T(8,128)S(1)}, f32[8,4096]{1,0:T(8,128)S(1)}, u32[]{:S(2)}, u32[]{:S(2)}) collective-permute-start(f32[8,4096]{1,0:T(8,128)S(1)} %get-tuple-element.42), channel_id=1, source_target_pairs={{0,8},{1,9},{2,10},{3,11},{4,12},{5,13},{6,14},{7,15},{8,0},{9,1},... | collective-permute-start | bytes 393224 | tf_op jit(solution)/shard_map/ppermute | solution.py:33
  19.6 7.1 %collective-permute-start.5 = (f32[8,3072]{1,0:T(8,128)S(1)}, f32[8,3072]{1,0:T(8,128)S(1)}, u32[]{:S(2)}, u32[]{:S(2)}) collective-permute-start(f32[8,3072]{1,0:T(8,128)S(1)} %get-tuple-element.45), channel_id=1, source_target_pairs={{0,8},{1,9},{2,10},{3,11},{4,12},{5,13},{6,14},{7,15},{8,0},{9,1},... | collective-permute-start | bytes 294920 | tf_op jit(solution)/shard_map/ppermute | solution.py:33
  25.2 1.6 %collective-permute-start.8 = (f32[8,4096]{1,0:T(8,128)S(1)}, f32[8,4096]{1,0:T(8,128)S(1)}, u32[]{:S(2)}, u32[]{:S(2)}) collective-permute-start(f32[8,4096]{1,0:T(8,128)S(1)} %get-tuple-element.61), channel_id=1, source_target_pairs={{0,4},{1,5},{2,6},{3,7},{4,0},{5,1},{6,2},{7,3},{8,12},{9,13},{10,... | collective-permute-start | bytes 393224 | tf_op jit(solution)/shard_map/ppermute | solution.py:33
  26.7 1.3 %collective-permute-start.6 = (f32[8,4096]{1,0:T(8,128)S(1)}, f32[8,4096]{1,0:T(8,128)S(1)}, u32[]{:S(2)}, u32[]{:S(2)}) collective-permute-start(f32[8,4096]{1,0:T(8,128)S(1)} %get-tuple-element.52), channel_id=1, source_target_pairs={{0,4},{1,5},{2,6},{3,7},{4,0},{5,1},{6,2},{7,3},{8,12},{9,13},{10,... | collective-permute-start | bytes 393224 | tf_op jit(solution)/shard_map/ppermute | solution.py:33
where the time goes:
time: 28.3 us; the launch traced here: 28.1 us
  waiting for transfers between devices  11.8 us (42%)
  Pallas kernels  8.8 us (31%)
  starting transfers between devices  7.49 us (26%)
    ppermute x9, waiting for transfers between devices, routed(): return lax.ppermute(block, AXES, pairs)  11.8 us
    ppermute x9, starting transfers between devices, routed(): return lax.ppermute(block, AXES, pairs)  7.49 us
    pallas_call x9, Pallas kernels, compute(): pl.pallas_call(kernel, out_shape=shapes, in_specs=[vmem] * len(args), out...  5.12 us
    pallas_call x1, Pallas kernels, two_chips(): pl.pallas_call(functools.partial(load_kernel, half), out_shape=[jax.Shape...  2.6 us
    pallas_call x2, Pallas kernels, written(): pl.pallas_call(functools.partial(write_kernel, half, into is not None), o...  1.08 us
  transfers between devices with their start and end apart: 9, of which 6 were waited for; matrix products, arithmetic and copies ran while one was open for 0% of the time, Pallas kernels for 23%

commit v1 on v0

--- a/solution.py
+++ b/solution.py
@@ -310,14 +310,15 @@
     return kept(a), kept(b), d, kept
 
 
-def outer_kernel(half, own, other, drive, got, mine, theirs, sent, ends, state):
+def outer_kernel(half, own, other, drive, got, sent, ends):
     core, chip = place()
     first = core == 0
     a, b, d, kept = outer_window(half, own, other, drive, got)
-    (f_a, g_a), (f_b, g_b) = start_of(a, d, kept), start_of(b, d, kept)
+    f_a, g_a = start_of(a, d, kept)
 
     @pl.when(chip == 0)
     def _():
+        f_b, g_b = start_of(b, d, kept)
         e_a = g_a + (f_a - g_a)
         e_b = kept(coarse_of(e_a, around(e_a), d)) + (f_b - g_b)
         frame = pltpu.roll(e_b, 16 - CUT, 0)[:8]
@@ -327,10 +328,21 @@
 
     @pl.when(chip > 0)
     def _():
+        ends[0:16, :] = f_a - g_a
+
+
+def outer_state_kernel(half, own, other, drive, got, mine, theirs, ends, state):
+    core, chip = place()
+    first = core == 0
+
+    @pl.when(chip > 0)
+    def _():
+        _, b, d, kept = outer_window(half, own, other, drive, got)
+        f_b, g_b = start_of(b, d, kept)
         rows = pl.ds(pl.multiple_of((half - WIDE) * core, 8), 16)
         before = picked(first, mine[rows, :], theirs[rows, :])
         d_rows = pl.ds(pl.multiple_of((2 * half - 16) * core, 8), 16)
-        fields = zip((f_a - g_a, f_b - g_b, d), (*before, drive[d_rows, :]))
+        fields = zip((ends[0:16, :], f_b - g_b, d), (*before, drive[d_rows, :]))
         for kind, (v, near) in enumerate(fields):
             top = jnp.where(first, v[:8], near[:8])
             mid = jnp.where(first, mixed(v[8:], near[:8]), mixed(near[8:], v[:8]))
@@ -338,9 +350,46 @@
             state[24 * kind : 24 * kind + 24, :] = jnp.concatenate([top, mid, low])
 
 
-def inner_end(half, left, right, drive, mine, theirs, keep, send, frame):
-    core, chip = place()
-    first = core == 0
+def near_end(
+    half,
+    left,
+    right,
+    middle,
+    drive,
+    mine,
+    theirs,
+    ends_left,
+    ends_right,
+    ends_middle,
+    ends_outer,
+    keep,
+    send,
+    frame,
+):
+    core, chip = place()
+    first = core == 0
+
+    def put(begin, e_a, e_b):
+        kept, sent = picked(first, e_a, e_b)
+        keep[pl.ds(begin, kept.shape[0]), :] = kept
+        send[pl.ds(begin, kept.shape[0]), :] = sent
+
+    @pl.when(chip == 0)
+    def _():
+        def rows(kind, begin, size):
+            into = pl.ds(half * kind + begin, size)
+            return jnp.concatenate([ends_left[into, :], ends_right[into, :]], axis=1)
+
+        def known(kind):
+            two = [field(ends_middle, kind, 2, 8 * i, 8)[...] for i in range(2)]
+            last = [field(ends_outer, kind, 2, 8 * i, 8)[...] for i in range(2)]
+            inner = rows(kind, 8, half - 16)
+            upper = jnp.concatenate([mixed(two[1], rows(kind, 0, 8)), inner])
+            lower = jnp.concatenate([inner, mixed(rows(kind, half - 8, 8), two[0])])
+            edge = jnp.where(first, mixed(last[1], two[0]), mixed(two[1], last[0]))
+            return jnp.concatenate([jnp.where(first, upper, lower), edge])
+
+        put(0, known(0), known(1))
 
     @pl.when(chip > 0)
     def _():
@@ -353,47 +402,16 @@
 
         whole = [across(i * mid, i * mid + mid) for i in range(count)]
         part = across(count * mid, left.shape[1], unfolded)
-        upper = [*whole, part]
-        lower = [pltpu.roll(part, 2, 0), *whole]
-        rows = jnp.concatenate([jnp.where(first, u, v) for u, v in zip(upper, lower)])
-        frame[...] = rows
-        current = pltpu.roll(jnp.concatenate([rows, rows[:8]]), CUT, 0)
-        into = pl.ds(pl.multiple_of(8 * (1 - core), 8), half)
-        d_a, d_b = picked(first, mine[into, :], theirs[into, :])
-        d = drive[pl.ds(inner_row(half, core), half), :]
-        e_a, e_b = chain(current, d_a, d_b, d)
-        put_ends(first, e_a[8 : half - 8], e_b[8 : half - 8], keep, send)
-
-
-def gather_kernel(half, ends_left, ends_right, middle, outer, near_keep, near_send, keep, send):
-    core, chip = place()
-    first = core == 0
-    near = half - 16
-
-    @pl.when(chip == 0)
-    def _():
-        def rows(kind, begin, size):
-            into = pl.ds(half * kind + begin, size)
-            return jnp.concatenate([ends_left[into, :], ends_right[into, :]], axis=1)
-
-        def known(kind):
-            two = [field(middle, kind, 2, 8 * i, 8)[...] for i in range(2)]
-            last = [field(outer, kind, 2, 8 * i, 8)[...] for i in range(2)]
-            beside = [rows(kind, 0, 8), rows(kind, half - 8, 8)]
-            return jnp.concatenate(
-                [
-                    rows(kind, 8, near),
-                    jnp.where(first, mixed(two[1], beside[0]), mixed(beside[1], two[0])),
-                    jnp.where(first, mixed(last[1], two[0]), mixed(two[1], last[0])),
-                ]
-            )
-
-        put_ends(first, known(0), known(1), keep, send)
-
-    @pl.when(chip > 0)
-    def _():
-        keep[0:near, :] = near_keep[...]
-        send[0:near, :] = near_send[...]
+        beside = middle[...]
+        upper = [beside, *whole, part]
+        lower = [pltpu.roll(part, 2, 0), *whole, beside]
+        rows = [jnp.where(first, u, v) for u, v in zip(upper, lower)]
+        frame[0:8, :] = jnp.where(first, rows[0], rows[-2])
+        frame[8:16, :] = jnp.where(first, rows[1], rows[-1])
+        current = pltpu.roll(jnp.concatenate([*rows, rows[0]]), CUT, 0)
+        d_a, d_b = picked(first, mine[...], theirs[...])
+        e_a, e_b = chain(current, d_a, d_b, drive[receiver_rows(half, core), :])
+        put(0, e_a[8:half], e_b[8:half])
 
 
 def put_ends(first, e_a, e_b, keep, send):
@@ -402,43 +420,18 @@
     send[...] = sent
 
 
-def middle_end(half, inner, middle, drive, mine, theirs, keep, send, current):
-    core, chip = place()
-    first = core == 0
-    last = inner.shape[0] - 16
+def outer_end(frame, outer, state, keep, send, current):
+    core, chip = place()
+    first = core == 0
 
     @pl.when((chip > 0) & first)
     def _():
-        current[...] = pltpu.roll(jnp.concatenate([middle[...], inner[0:16, :]]), CUT, 0)
+        part = pltpu.roll(unfolded(outer[...]), 2, 0)
+        current[...] = pltpu.roll(jnp.concatenate([part, frame[...]]), CUT, 0)
 
     @pl.when((chip > 0) & (core == 1))
     def _():
-        rows = jnp.concatenate([inner[last : last + 16, :], middle[...]])
-        current[...] = pltpu.roll(rows, 24 - CUT, 0)
-
-    @pl.when(chip > 0)
-    def _():
-        rows = pl.ds(pl.multiple_of((half - 16) * core, 8), 24)
-        d_a, d_b = picked(first, mine[rows, :], theirs[rows, :])
-        d = drive[pl.ds(pl.multiple_of((2 * half - 24) * core, 8), 24), :]
-        e_a, e_b = chain(current[...], d_a, d_b, d)
-        put_ends(first, e_a[8:16], e_b[8:16], keep, send)
-
-
-def outer_end(inner, middle, outer, state, keep, send, current):
-    core, chip = place()
-    first = core == 0
-    last = inner.shape[0] - 8
-
-    @pl.when((chip > 0) & first)
-    def _():
-        part = pltpu.roll(unfolded(outer[...]), 2, 0)
-        rows = jnp.concatenate([part, middle[...], inner[0:8, :]])
-        current[...] = pltpu.roll(rows, CUT, 0)
-
-    @pl.when((chip > 0) & (core == 1))
-    def _():
-        rows = jnp.concatenate([inner[last : last + 8, :], middle[...], unfolded(outer[...])])
+        rows = jnp.concatenate([frame[...], unfolded(outer[...])])
         current[...] = pltpu.roll(rows, 24 - CUT, 0)
 
     @pl.when(chip > 0)
@@ -456,14 +449,15 @@
 
 
 def write_kernel(half, last, *refs):
-    pieces, out, sems = refs[: 1 if last else 5], refs[-2], refs[-1]
-    core, chip = place()
+    pieces, out, sems = refs[: 1 if last else 3], refs[-2], refs[-1]
+    core, chip = place()
+    near = half - 8
 
     def copy_all(order):
         copies = []
-        for i, (mine, part, source, begin, size) in enumerate(order):
-            upper = (16, 8, 0)[part]
-            lower = (half, 2 * half - 16, 2 * half - 8)[part]
+        for i, (mine, part, source, begin) in enumerate(order):
+            size = (near, 8)[part]
+            upper, lower = ((8, half), (0, 2 * half - 8))[part]
             row = pl.multiple_of(jnp.where((core == 0) == mine, upper, lower), 8)
             copy = pltpu.make_async_copy(
                 pieces[source].at[pl.ds(begin, size), :],
@@ -479,29 +473,17 @@
 
         @pl.when(chip > 0)
         def _():
-            copy_all(((False, 2, 0, 0, 8),))
+            copy_all(((False, 1, 0, 0),))
 
     else:
-        near = half - 16
 
         @pl.when(chip == 0)
         def _():
-            parts = ((0, 0, near), (1, near, 8), (2, near + 8, 8))
-            copy_all(
-                [(mine, part, source, *rows) for mine, source in ((True, 0), (False, 1)) for part, *rows in parts]
-            )
+            copy_all(((True, 0, 0, 0), (False, 0, 1, 0), (True, 1, 0, near), (False, 1, 1, near)))
 
         @pl.when(chip > 0)
         def _():
-            copy_all(
-                (
-                    (True, 0, 0, 0, near),
-                    (False, 0, 1, 0, near),
-                    (True, 1, 2, 0, 8),
-                    (False, 1, 3, 0, 8),
-                    (True, 2, 4, 0, 8),
-                )
-            )
+            copy_all(((True, 0, 0, 0), (False, 0, 1, 0), (True, 1, 2, 0)))
 
 
 def written(half, pieces, shape, into=None):
@@ -646,40 +628,46 @@
     )
     here_2 = routed(sent_2, stage_swap(0))
     (delta_other,) = compute(
-        functools.partial(state_kernel, half), [(half + WIDE, width)], (other, after(held, sent_2))
-    )
-    sent_3, ends_3, state_3 = compute(
+        functools.partial(state_kernel, half),
+        [(half + WIDE, width)],
+        (other, after(held, sent_2)),
+    )
+    sent_3, ends_3 = compute(
         functools.partial(outer_kernel, half),
-        [(8, width * 3 // 4), (32, width), (3 * 24, width)],
-        (own, other, held, got, delta_own, delta_other),
+        [(8, width * 3 // 4), (32, width)],
+        (own, other, after(held, delta_other), got),
     )
     here_3 = routed(sent_3, stage_swap(0))
-    near_keep, near_send, frame = compute(
-        functools.partial(inner_end, half),
-        [(half - 16, width), (half - 16, width), (half - 8, width)],
-        (here_l, here_r, held, delta_own, after(delta_other, sent_3)),
-    )
-    keep_1, send_1 = compute(
-        functools.partial(gather_kernel, half),
-        [(half, width)] * 2,
-        (ends_l, ends_r, ends_2, ends_3, near_keep, near_send),
+    (state_3,) = compute(
+        functools.partial(outer_state_kernel, half),
+        [(3 * 24, width)],
+        (own, other, held, got, delta_own, delta_other, ends_3),
+    )
+    keep_1, send_1, frame = compute(
+        functools.partial(near_end, half),
+        [(half, width), (half, width), (16, width)],
+        (
+            here_l,
+            here_r,
+            here_2,
+            held,
+            delta_own,
+            after(delta_other, state_3),
+            ends_l,
+            ends_r,
+            ends_2,
+            ends_3,
+        ),
     )
     back_1 = routed(send_1, partner)
-    keep_2, send_2 = compute(
-        functools.partial(middle_end, half),
-        [(8, width)] * 2,
-        (frame, here_2, held, delta_own, after(delta_other, state_3)),
-        scratch_shapes=[pltpu.VMEM((24, width), jnp.float32)],
-    )
-    back_2 = routed(send_2, partner)
     keep_3, send_3 = compute(
         outer_end,
         [(8, width)] * 2,
-        (frame, here_2, here_3, after(state_3, keep_2)),
+        (frame, here_3, state_3),
         scratch_shapes=[pltpu.VMEM((24, width), jnp.float32)],
     )
     back_3 = routed(send_3, partner)
-    out = written(half, (keep_1, back_1, keep_2, back_2, keep_3), starts.shape)
+    out = written(half, (keep_1, back_1, keep_3), starts.shape)
     return written(half, (back_3,), starts.shape, into=out)
 
 

time: 28.3 us -> 28.3 us (level)
  starting transfers between devices: 7.49 us -> 6.72 us
  waiting for transfers between devices: 11.8 us -> 12.5 us
    ppermute x9 -> x8, waiting for transfers between devices: 11.8 us -> 12.5 us  [routed(): return lax.ppermute(block, AXES, pairs)]
    ppermute x9 -> x8, starting transfers between devices: 7.49 us -> 6.72 us  [routed(): return lax.ppermute(block, AXES, pairs)]
    pallas_call x9 -> x8, Pallas kernels: 5.12 us -> 5.16 us  [compute(): pl.pallas_call(kernel, out_shape=shapes, in_specs=[vmem] * len(args), out...]
  transfers between devices with their start and end apart: 9 -> 8, of which waited for: 6 -> 4; matrix products, arithmetic and copies ran while one was open for 0% -> 0% of each run, Pallas kernels for 23% -> 23%
where the time goes in v1:
time: 28.3 us; the launch traced here: 28.2 us
  waiting for transfers between devices  12.5 us (44%)
  Pallas kernels  8.84 us (31%)
  starting transfers between devices  6.72 us (24%)
    ppermute x8, waiting for transfers between devices, routed(): return lax.ppermute(block, AXES, pairs)  12.5 us
    ppermute x8, starting transfers between devices, routed(): return lax.ppermute(block, AXES, pairs)  6.72 us
    pallas_call x8, Pallas kernels, compute(): pl.pallas_call(kernel, out_shape=shapes, in_specs=[vmem] * len(args), out...  5.16 us
    pallas_call x1, Pallas kernels, two_chips(): pl.pallas_call(functools.partial(load_kernel, half), out_shape=[jax.Shape...  2.6 us
    pallas_call x2, Pallas kernels, written(): pl.pallas_call(functools.partial(write_kernel, half, into is not None), o...  1.08 us
  transfers between devices with their start and end apart: 8, of which 4 were waited for; matrix products, arithmetic and copies ran while one was open for 0% of the time, Pallas kernels for 23%

profile of v1, /device:TPU:0, one launch (start us, length us, event | category | flops | bytes accessed | tf_op | source)
XLA Modules:
  0.0 28.2 jit_solution(15926223278143044333)
XLA Ops:
  0.0 0.5 %collective-permute-start = (f32[64,4096]{1,0:T(8,128)}, f32[64,4096]{1,0:T(8,128)S(1)}, u32[]{:S(2)}, u32[]{:S(2)}) collective-permute-start(f32[64,4096]{1,0:T(8,128)} %bitcast.1), channel_id=1, source_target_pairs={{0,4},{1,5},{2,6},{3,7},{4,0},{5,1},{6,2},{7,3},{8,12},{9,13},{10,... | collective-permute-start | bytes 3145736 | tf_op jit(solution)/shard_map/ppermute | solution.py:33
  0.5 2.6 %load.1 = (f32[64,4096]{1,0:T(8,128)S(1)}, f32[64,4096]{1,0:T(8,128)S(1)}, f32[64,4096]{1,0:T(8,128)S(1)}) custom-call(f32[1,64,4096]{2,1,0:T(8,128)} %starts.1, f32[64,4096]{1,0:T(8,128)} %drive.1), custom_call_target="tpu_custom_call" | custom-call | flops 5898240 | bytes 4194304 | tf_op jit(solution)/shard_map/load/pallas_call | solution.py:595
  3.1 0.0 collective-permute-done.other
  3.1 1.0 %shard_map.28 = (f32[8,5632]{1,0:T(8,128)S(1)}, f32[64,2048]{1,0:T(8,128)S(1)}) custom-call(f32[64,4096]{1,0:T(8,128)S(1)} %get-tuple-element.28.own, f32[64,4096]{1,0:T(8,128)S(1)} %collective-permute-done.other, f32[64,4096]{1,0:T(8,128)S(1)} %get-tuple-element.39.drive, f32[64,4096]{1,0:T(8,128)S(1)} %get-tuple-element.32.mine), custom_call_target="tpu_custom_call" | custom-call | tf_op jit(solution)/shard_map/pallas_call | solution.py:90
  4.1 1.1 %shard_map.29 = (f32[8,5632]{1,0:T(8,128)S(1)}, f32[64,2048]{1,0:T(8,128)S(1)}, f32[8,9216]{1,0:T(8,128)S(1)}) custom-call(f32[64,4096]{1,0:T(8,128)S(1)} %get-tuple-element.28.own, f32[64,4096]{1,0:T(8,128)S(1)} %collective-permute-done.other, f32[64,4096]{1,0:T(8,128)S(1)} %get-tuple-element.39.drive, f32[64,4096]{1,0:T(8,128)S(1)} %get-tuple-element.32.mine), custom_call_target="tpu_custom_call" | custom-call | tf_op jit(solution)/shard_map/pallas_call | solution.py:90
  5.2 2.8 %collective-permute-start.4 = (f32[8,9216]{1,0:T(8,128)S(1)}, f32[8,9216]{1,0:T(8,128)S(1)}, u32[]{:S(2)}, u32[]{:S(2)}) collective-permute-start(f32[8,9216]{1,0:T(8,128)S(1)} %get-tuple-element.38), channel_id=1, source_target_pairs={{0,16},{1,4},{2,5},{3,6},{4,1},{5,2},{6,3},{7,23},{8,24},{9,12},{1... | collective-permute-start | bytes 884744 | tf_op jit(solution)/shard_map/ppermute | solution.py:33
  8.0 0.0 collective-permute-start.2
  8.0 2.0 %collective-permute-start.1 = (f32[8,5632]{1,0:T(8,128)S(1)}, f32[8,5632]{1,0:T(8,128)S(1)}, u32[]{:S(2)}, u32[]{:S(2)}) collective-permute-start(f32[8,5632]{1,0:T(8,128)S(1)} %get-tuple-element.31), channel_id=1, source_target_pairs={{0,8},{1,9},{2,10},{3,11},{4,12},{5,13},{6,14},{7,15},{8,0},{9,1},... | collective-permute-start | bytes 540680 | tf_op jit(solution)/shard_map/ppermute | solution.py:33
  10.0 1.4 %shard_map.30 = (f32[8,4096]{1,0:T(8,128)S(1)}, f32[32,4096]{1,0:T(8,128)S(1)}, f32[40,4096]{1,0:T(8,128)S(1)}) custom-call(f32[64,4096]{1,0:T(8,128)S(1)} %get-tuple-element.28.own, f32[64,4096]{1,0:T(8,128)S(1)} %collective-permute-done.other, f32[64,4096]{1,0:T(8,128)S(1)} %get-tuple-element.39.drive), custom_call_target="tpu_custom_call" | custom-call | tf_op jit(solution)/shard_map/pallas_call | solution.py:90
  11.4 0.2 collective-permute-start.3
  11.6 1.1 %collective-permute-done.4.got = f32[8,9216]{1,0:T(8,128)S(1)} collective-permute-done((f32[8,9216]{1,0:T(8,128)S(1)}, f32[8,9216]{1,0:T(8,128)S(1)}, u32[]{:S(2)}, u32[]{:S(2)}) %collective-permute-start.4) | collective-permute-done | bytes 294944 | tf_op jit(solution)/shard_map/ppermute | solution.py:33
  12.7 1.5 %shard_map.32 = (f32[8,3072]{1,0:T(8,128)S(1)}, f32[32,4096]{1,0:T(8,128)S(1)}) custom-call(f32[64,4096]{1,0:T(8,128)S(1)} %get-tuple-element.28.own, f32[64,4096]{1,0:T(8,128)S(1)} %collective-permute-done.other, f32[64,4096]{1,0:T(8,128)S(1)} %get-tuple-element.39.drive, f32[8,9216]{1,0:T(8,128)S(1)} %collective-permute-done.4.got), custom_call_target="tpu_custom_call" | custom-call | tf_op jit(solution)/shard_map/pallas_call | solution.py:90
  14.2 7.0 %collective-permute-done.3.middle = f32[8,4096]{1,0:T(8,128)S(1)} collective-permute-done((f32[8,4096]{1,0:T(8,128)S(1)}, f32[8,4096]{1,0:T(8,128)S(1)}, u32[]{:S(2)}, u32[]{:S(2)}) %collective-permute-start.3) | collective-permute-done | bytes 131104 | tf_op jit(solution)/shard_map/ppermute | solution.py:33
  21.3 0.0 collective-permute-done.2.right
  21.3 0.0 collective-permute-done.1.left
  21.3 0.2 shard_map.34
  21.5 0.1 collective-permute-start.7
  21.6 1.1 %collective-permute-start.5 = (f32[8,3072]{1,0:T(8,128)S(1)}, f32[8,3072]{1,0:T(8,128)S(1)}, u32[]{:S(2)}, u32[]{:S(2)}) collective-permute-start(f32[8,3072]{1,0:T(8,128)S(1)} %get-tuple-element.46), channel_id=1, source_target_pairs={{0,8},{1,9},{2,10},{3,11},{4,12},{5,13},{6,14},{7,15},{8,0},{9,1},... | collective-permute-start | bytes 294920 | tf_op jit(solution)/shard_map/ppermute | solution.py:33
  22.7 4.1 %collective-permute-done.5.outer = f32[8,3072]{1,0:T(8,128)S(1)} collective-permute-done((f32[8,3072]{1,0:T(8,128)S(1)}, f32[8,3072]{1,0:T(8,128)S(1)}, u32[]{:S(2)}, u32[]{:S(2)}) %collective-permute-start.5) | collective-permute-done | bytes 98336 | tf_op jit(solution)/shard_map/ppermute | solution.py:33
  26.8 0.0 collective-permute-start.6
  26.8 0.0 collective-permute-done.7.refs_1_
  26.8 1.0 %shard_map.36.refs_1_ = f32[1,64,4096]{2,1,0:T(8,128)} custom-call(f32[32,4096]{1,0:T(8,128)S(1)} %get-tuple-element.48.refs_0_, f32[32,4096]{1,0:T(8,128)S(1)} %collective-permute-done.7.refs_1_, f32[8,4096]{1,0:T(8,128)S(1)} %get-tuple-element.50.refs_2_), custom_call_target="tpu_custom_call" | custom-call | tf_op jit(solution)/shard_map/pallas_call | solution.py:492
  27.8 0.3 %collective-permute-done.6.refs_0_ = f32[8,4096]{1,0:T(8,128)S(1)} collective-permute-done((f32[8,4096]{1,0:T(8,128)S(1)}, f32[8,4096]{1,0:T(8,128)S(1)}, u32[]{:S(2)}, u32[]{:S(2)}) %collective-permute-start.6) | collective-permute-done | bytes 131104 | tf_op jit(solution)/shard_map/ppermute | solution.py:33
  28.1 0.1 shard_map.37
  (3 shorter events, 0.0 us)
Async XLA Ops:
  0.0 3.1 %collective-permute-start = (f32[64,4096]{1,0:T(8,128)}, f32[64,4096]{1,0:T(8,128)S(1)}, u32[]{:S(2)}, u32[]{:S(2)}) collective-permute-start(f32[64,4096]{1,0:T(8,128)} %bitcast.1), channel_id=1, source_target_pairs={{0,4},{1,5},{2,6},{3,7},{4,0},{5,1},{6,2},{7,3},{8,12},{9,13},{10,... | collective-permute-start | bytes 3145736 | tf_op jit(solution)/shard_map/ppermute | solution.py:33
  5.2 7.5 %collective-permute-start.4 = (f32[8,9216]{1,0:T(8,128)S(1)}, f32[8,9216]{1,0:T(8,128)S(1)}, u32[]{:S(2)}, u32[]{:S(2)}) collective-permute-start(f32[8,9216]{1,0:T(8,128)S(1)} %get-tuple-element.38), channel_id=1, source_target_pairs={{0,16},{1,4},{2,5},{3,6},{4,1},{5,2},{6,3},{7,23},{8,24},{9,12},{1... | collective-permute-start | bytes 884744 | tf_op jit(solution)/shard_map/ppermute | solution.py:33
  8.0 13.3 %collective-permute-start.2 = (f32[8,5632]{1,0:T(8,128)S(1)}, f32[8,5632]{1,0:T(8,128)S(1)}, u32[]{:S(2)}, u32[]{:S(2)}) collective-permute-start(f32[8,5632]{1,0:T(8,128)S(1)} %get-tuple-element.33), channel_id=1, source_target_pairs={{0,8},{1,9},{2,10},{3,11},{4,12},{5,13},{6,14},{7,15},{8,0},{9,1},... | collective-permute-start | bytes 540680 | tf_op jit(solution)/shard_map/ppermute | solution.py:33
  8.0 13.3 %collective-permute-start.1 = (f32[8,5632]{1,0:T(8,128)S(1)}, f32[8,5632]{1,0:T(8,128)S(1)}, u32[]{:S(2)}, u32[]{:S(2)}) collective-permute-start(f32[8,5632]{1,0:T(8,128)S(1)} %get-tuple-element.31), channel_id=1, source_target_pairs={{0,8},{1,9},{2,10},{3,11},{4,12},{5,13},{6,14},{7,15},{8,0},{9,1},... | collective-permute-start | bytes 540680 | tf_op jit(solution)/shard_map/ppermute | solution.py:33
  11.4 9.9 %collective-permute-start.3 = (f32[8,4096]{1,0:T(8,128)S(1)}, f32[8,4096]{1,0:T(8,128)S(1)}, u32[]{:S(2)}, u32[]{:S(2)}) collective-permute-start(f32[8,4096]{1,0:T(8,128)S(1)} %get-tuple-element.35), channel_id=1, source_target_pairs={{0,8},{1,9},{2,10},{3,11},{4,12},{5,13},{6,14},{7,15},{8,0},{9,1},... | collective-permute-start | bytes 393224 | tf_op jit(solution)/shard_map/ppermute | solution.py:33
  21.5 5.3 %collective-permute-start.7 = (f32[32,4096]{1,0:T(8,128)S(1)}, f32[32,4096]{1,0:T(8,128)S(1)}, u32[]{:S(2)}, u32[]{:S(2)}) collective-permute-start(f32[32,4096]{1,0:T(8,128)S(1)} %get-tuple-element.49), channel_id=1, source_target_pairs={{0,4},{1,5},{2,6},{3,7},{4,0},{5,1},{6,2},{7,3},{8,12},{9,13},{10,... | collective-permute-start | bytes 1572872 | tf_op jit(solution)/shard_map/ppermute | solution.py:33
  21.6 5.2 %collective-permute-start.5 = (f32[8,3072]{1,0:T(8,128)S(1)}, f32[8,3072]{1,0:T(8,128)S(1)}, u32[]{:S(2)}, u32[]{:S(2)}) collective-permute-start(f32[8,3072]{1,0:T(8,128)S(1)} %get-tuple-element.46), channel_id=1, source_target_pairs={{0,8},{1,9},{2,10},{3,11},{4,12},{5,13},{6,14},{7,15},{8,0},{9,1},... | collective-permute-start | bytes 294920 | tf_op jit(solution)/shard_map/ppermute | solution.py:33
  26.8 1.3 %collective-permute-start.6 = (f32[8,4096]{1,0:T(8,128)S(1)}, f32[8,4096]{1,0:T(8,128)S(1)}, u32[]{:S(2)}, u32[]{:S(2)}) collective-permute-start(f32[8,4096]{1,0:T(8,128)S(1)} %get-tuple-element.47), channel_id=1, source_target_pairs={{0,4},{1,5},{2,6},{3,7},{4,0},{5,1},{6,2},{7,3},{8,12},{9,13},{10,... | collective-permute-start | bytes 393224 | tf_op jit(solution)/shard_map/ppermute | solution.py:33

commit v2 on v0

--- a/solution.py
+++ b/solution.py
@@ -310,14 +310,15 @@
     return kept(a), kept(b), d, kept
 
 
-def outer_kernel(half, own, other, drive, got, mine, theirs, sent, ends, state):
+def outer_kernel(half, own, other, drive, got, sent, ends):
     core, chip = place()
     first = core == 0
     a, b, d, kept = outer_window(half, own, other, drive, got)
-    (f_a, g_a), (f_b, g_b) = start_of(a, d, kept), start_of(b, d, kept)
+    f_a, g_a = start_of(a, d, kept)
 
     @pl.when(chip == 0)
     def _():
+        f_b, g_b = start_of(b, d, kept)
         e_a = g_a + (f_a - g_a)
         e_b = kept(coarse_of(e_a, around(e_a), d)) + (f_b - g_b)
         frame = pltpu.roll(e_b, 16 - CUT, 0)[:8]
@@ -327,10 +328,21 @@
 
     @pl.when(chip > 0)
     def _():
+        ends[0:16, :] = f_a - g_a
+
+
+def outer_state_kernel(half, own, other, drive, got, mine, theirs, ends, state):
+    core, chip = place()
+    first = core == 0
+
+    @pl.when(chip > 0)
+    def _():
+        _, b, d, kept = outer_window(half, own, other, drive, got)
+        f_b, g_b = start_of(b, d, kept)
         rows = pl.ds(pl.multiple_of((half - WIDE) * core, 8), 16)
         before = picked(first, mine[rows, :], theirs[rows, :])
         d_rows = pl.ds(pl.multiple_of((2 * half - 16) * core, 8), 16)
-        fields = zip((f_a - g_a, f_b - g_b, d), (*before, drive[d_rows, :]))
+        fields = zip((ends[0:16, :], f_b - g_b, d), (*before, drive[d_rows, :]))
         for kind, (v, near) in enumerate(fields):
             top = jnp.where(first, v[:8], near[:8])
             mid = jnp.where(first, mixed(v[8:], near[:8]), mixed(near[8:], v[:8]))
@@ -648,16 +660,21 @@
     (delta_other,) = compute(
         functools.partial(state_kernel, half), [(half + WIDE, width)], (other, after(held, sent_2))
     )
-    sent_3, ends_3, state_3 = compute(
+    sent_3, ends_3 = compute(
         functools.partial(outer_kernel, half),
-        [(8, width * 3 // 4), (32, width), (3 * 24, width)],
-        (own, other, held, got, delta_own, delta_other),
+        [(8, width * 3 // 4), (32, width)],
+        (own, other, after(held, delta_other), got),
     )
     here_3 = routed(sent_3, stage_swap(0))
+    (state_3,) = compute(
+        functools.partial(outer_state_kernel, half),
+        [(3 * 24, width)],
+        (own, other, held, got, delta_own, delta_other, ends_3),
+    )
     near_keep, near_send, frame = compute(
         functools.partial(inner_end, half),
         [(half - 16, width), (half - 16, width), (half - 8, width)],
-        (here_l, here_r, held, delta_own, after(delta_other, sent_3)),
+        (here_l, here_r, held, delta_own, after(delta_other, state_3)),
     )
     keep_1, send_1 = compute(
         functools.partial(gather_kernel, half),
@@ -668,7 +685,7 @@
     keep_2, send_2 = compute(
         functools.partial(middle_end, half),
         [(8, width)] * 2,
-        (frame, here_2, held, delta_own, after(delta_other, state_3)),
+        (frame, here_2, held, delta_own, delta_other),
         scratch_shapes=[pltpu.VMEM((24, width), jnp.float32)],
     )
     back_2 = routed(send_2, partner)

time: 28.3 us -> 28.3 us (level)
    pallas_call x9 -> x10, Pallas kernels: 5.12 us -> 5.15 us  [compute(): pl.pallas_call(kernel, out_shape=shapes, in_specs=[vmem] * len(args), out...]
where the time goes in v2:
time: 28.3 us; the launch traced here: 28.1 us
  waiting for transfers between devices  11.7 us (41%)
  Pallas kernels  8.83 us (31%)
  starting transfers between devices  7.49 us (26%)
    ppermute x9, waiting for transfers between devices, routed(): return lax.ppermute(block, AXES, pairs)  11.7 us
    ppermute x9, starting transfers between devices, routed(): return lax.ppermute(block, AXES, pairs)  7.49 us
    pallas_call x10, Pallas kernels, compute(): pl.pallas_call(kernel, out_shape=shapes, in_specs=[vmem] * len(args), out...  5.15 us
    pallas_call x1, Pallas kernels, two_chips(): pl.pallas_call(functools.partial(load_kernel, half), out_shape=[jax.Shape...  2.6 us
    pallas_call x2, Pallas kernels, written(): pl.pallas_call(functools.partial(write_kernel, half, into is not None), o...  1.08 us
  transfers between devices with their start and end apart: 9, of which 6 were waited for; matrix products, arithmetic and copies ran while one was open for 0% of the time, Pallas kernels for 23%

profile of v2, /device:TPU:0, one launch (start us, length us, event | category | flops | bytes accessed | tf_op | source)
XLA Modules:
  0.0 28.1 jit_solution(1324942922386767726)
XLA Ops:
  0.0 0.5 %collective-permute-start = (f32[64,4096]{1,0:T(8,128)}, f32[64,4096]{1,0:T(8,128)S(1)}, u32[]{:S(2)}, u32[]{:S(2)}) collective-permute-start(f32[64,4096]{1,0:T(8,128)} %bitcast.1), channel_id=1, source_target_pairs={{0,4},{1,5},{2,6},{3,7},{4,0},{5,1},{6,2},{7,3},{8,12},{9,13},{10,... | collective-permute-start | bytes 3145736 | tf_op jit(solution)/shard_map/ppermute | solution.py:33
  0.5 2.6 %load.1 = (f32[64,4096]{1,0:T(8,128)S(1)}, f32[64,4096]{1,0:T(8,128)S(1)}, f32[64,4096]{1,0:T(8,128)S(1)}) custom-call(f32[1,64,4096]{2,1,0:T(8,128)} %starts.1, f32[64,4096]{1,0:T(8,128)} %drive.1), custom_call_target="tpu_custom_call" | custom-call | flops 5898240 | bytes 4194304 | tf_op jit(solution)/shard_map/load/pallas_call | solution.py:625
  3.1 0.0 collective-permute-done.other
  3.1 1.0 %shard_map.28 = (f32[8,5632]{1,0:T(8,128)S(1)}, f32[64,2048]{1,0:T(8,128)S(1)}) custom-call(f32[64,4096]{1,0:T(8,128)S(1)} %get-tuple-element.33.own, f32[64,4096]{1,0:T(8,128)S(1)} %collective-permute-done.other, f32[64,4096]{1,0:T(8,128)S(1)} %get-tuple-element.44.drive, f32[64,4096]{1,0:T(8,128)S(1)} %get-tuple-element.37.mine), custom_call_target="tpu_custom_call" | custom-call | tf_op jit(solution)/shard_map/pallas_call | solution.py:90
  4.1 1.1 %shard_map.29 = (f32[8,5632]{1,0:T(8,128)S(1)}, f32[64,2048]{1,0:T(8,128)S(1)}, f32[8,9216]{1,0:T(8,128)S(1)}) custom-call(f32[64,4096]{1,0:T(8,128)S(1)} %get-tuple-element.33.own, f32[64,4096]{1,0:T(8,128)S(1)} %collective-permute-done.other, f32[64,4096]{1,0:T(8,128)S(1)} %get-tuple-element.44.drive, f32[64,4096]{1,0:T(8,128)S(1)} %get-tuple-element.37.mine), custom_call_target="tpu_custom_call" | custom-call | tf_op jit(solution)/shard_map/pallas_call | solution.py:90
  5.2 2.8 %collective-permute-start.3 = (f32[8,9216]{1,0:T(8,128)S(1)}, f32[8,9216]{1,0:T(8,128)S(1)}, u32[]{:S(2)}, u32[]{:S(2)}) collective-permute-start(f32[8,9216]{1,0:T(8,128)S(1)} %get-tuple-element.43), channel_id=1, source_target_pairs={{0,16},{1,4},{2,5},{3,6},{4,1},{5,2},{6,3},{7,23},{8,24},{9,12},{1... | collective-permute-start | bytes 884744 | tf_op jit(solution)/shard_map/ppermute | solution.py:33
  8.0 0.0 collective-permute-start.2
  8.0 2.0 %collective-permute-start.1 = (f32[8,5632]{1,0:T(8,128)S(1)}, f32[8,5632]{1,0:T(8,128)S(1)}, u32[]{:S(2)}, u32[]{:S(2)}) collective-permute-start(f32[8,5632]{1,0:T(8,128)S(1)} %get-tuple-element.36), channel_id=1, source_target_pairs={{0,8},{1,9},{2,10},{3,11},{4,12},{5,13},{6,14},{7,15},{8,0},{9,1},... | collective-permute-start | bytes 540680 | tf_op jit(solution)/shard_map/ppermute | solution.py:33
  10.0 1.4 %shard_map.30 = (f32[8,4096]{1,0:T(8,128)S(1)}, f32[32,4096]{1,0:T(8,128)S(1)}, f32[40,4096]{1,0:T(8,128)S(1)}) custom-call(f32[64,4096]{1,0:T(8,128)S(1)} %get-tuple-element.33.own, f32[64,4096]{1,0:T(8,128)S(1)} %collective-permute-done.other, f32[64,4096]{1,0:T(8,128)S(1)} %get-tuple-element.44.drive), custom_call_target="tpu_custom_call" | custom-call | tf_op jit(solution)/shard_map/pallas_call | solution.py:90
  11.4 1.3 %collective-permute-done.3.got = f32[8,9216]{1,0:T(8,128)S(1)} collective-permute-done((f32[8,9216]{1,0:T(8,128)S(1)}, f32[8,9216]{1,0:T(8,128)S(1)}, u32[]{:S(2)}, u32[]{:S(2)}) %collective-permute-start.3) | collective-permute-done | bytes 294944 | tf_op jit(solution)/shard_map/ppermute | solution.py:33
  12.7 1.5 %shard_map.32 = (f32[8,3072]{1,0:T(8,128)S(1)}, f32[32,4096]{1,0:T(8,128)S(1)}) custom-call(f32[64,4096]{1,0:T(8,128)S(1)} %get-tuple-element.33.own, f32[64,4096]{1,0:T(8,128)S(1)} %collective-permute-done.other, f32[64,4096]{1,0:T(8,128)S(1)} %get-tuple-element.44.drive, f32[8,9216]{1,0:T(8,128)S(1)} %collective-permute-done.3.got), custom_call_target="tpu_custom_call" | custom-call | tf_op jit(solution)/shard_map/pallas_call | solution.py:90
  14.2 1.2 %collective-permute-done.2.right = f32[8,5632]{1,0:T(8,128)S(1)} collective-permute-done((f32[8,5632]{1,0:T(8,128)S(1)}, f32[8,5632]{1,0:T(8,128)S(1)}, u32[]{:S(2)}, u32[]{:S(2)}) %collective-permute-start.2) | collective-permute-done | bytes 180256 | tf_op jit(solution)/shard_map/ppermute | solution.py:33
  15.4 3.1 %collective-permute-done.1.left = f32[8,5632]{1,0:T(8,128)S(1)} collective-permute-done((f32[8,5632]{1,0:T(8,128)S(1)}, f32[8,5632]{1,0:T(8,128)S(1)}, u32[]{:S(2)}, u32[]{:S(2)}) %collective-permute-start.1) | collective-permute-done | bytes 180256 | tf_op jit(solution)/shard_map/ppermute | solution.py:33
  18.5 0.2 shard_map.37
  18.6 0.1 collective-permute-start.7
  18.7 0.9 %collective-permute-start.4 = (f32[8,4096]{1,0:T(8,128)S(1)}, f32[8,4096]{1,0:T(8,128)S(1)}, u32[]{:S(2)}, u32[]{:S(2)}) collective-permute-start(f32[8,4096]{1,0:T(8,128)S(1)} %get-tuple-element.41), channel_id=1, source_target_pairs={{0,8},{1,9},{2,10},{3,11},{4,12},{5,13},{6,14},{7,15},{8,0},{9,1},... | collective-permute-start | bytes 393224 | tf_op jit(solution)/shard_map/ppermute | solution.py:33
  19.6 1.2 %collective-permute-start.5 = (f32[8,3072]{1,0:T(8,128)S(1)}, f32[8,3072]{1,0:T(8,128)S(1)}, u32[]{:S(2)}, u32[]{:S(2)}) collective-permute-start(f32[8,3072]{1,0:T(8,128)S(1)} %get-tuple-element.48), channel_id=1, source_target_pairs={{0,8},{1,9},{2,10},{3,11},{4,12},{5,13},{6,14},{7,15},{8,0},{9,1},... | collective-permute-start | bytes 294920 | tf_op jit(solution)/shard_map/ppermute | solution.py:33
  20.8 4.3 %collective-permute-done.4.middle = f32[8,4096]{1,0:T(8,128)S(1)} collective-permute-done((f32[8,4096]{1,0:T(8,128)S(1)}, f32[8,4096]{1,0:T(8,128)S(1)}, u32[]{:S(2)}, u32[]{:S(2)}) %collective-permute-start.4) | collective-permute-done | bytes 131104 | tf_op jit(solution)/shard_map/ppermute | solution.py:33
  25.2 0.0 collective-permute-start.8
  25.2 1.6 %collective-permute-done.5.outer = f32[8,3072]{1,0:T(8,128)S(1)} collective-permute-done((f32[8,3072]{1,0:T(8,128)S(1)}, f32[8,3072]{1,0:T(8,128)S(1)}, u32[]{:S(2)}, u32[]{:S(2)}) %collective-permute-start.5) | collective-permute-done | bytes 98336 | tf_op jit(solution)/shard_map/ppermute | solution.py:33
  26.7 0.0 collective-permute-start.6
  26.7 0.0 collective-permute-done.8.refs_3_
  26.7 0.0 collective-permute-done.7.refs_1_
  26.7 1.0 %shard_map.38.refs_1_ = f32[1,64,4096]{2,1,0:T(8,128)} custom-call(f32[32,4096]{1,0:T(8,128)S(1)} %get-tuple-element.57.refs_0_, f32[32,4096]{1,0:T(8,128)S(1)} %collective-permute-done.7.refs_1_, f32[8,4096]{1,0:T(8,128)S(1)} %get-tuple-element.49.refs_2_, f32[8,4096]{1,0:T(8,128)S(1)} %collective-permute-done.8.refs_3_, ...), custom_call_target="tpu_custom_call" | custom-call | tf_op jit(solution)/shard_map/pallas_call | solution.py:522
  27.8 0.3 %collective-permute-done.6.refs_0_ = f32[8,4096]{1,0:T(8,128)S(1)} collective-permute-done((f32[8,4096]{1,0:T(8,128)S(1)}, f32[8,4096]{1,0:T(8,128)S(1)}, u32[]{:S(2)}, u32[]{:S(2)}) %collective-permute-start.6) | collective-permute-done | bytes 131104 | tf_op jit(solution)/shard_map/ppermute | solution.py:33
  28.1 0.1 shard_map.39
  (5 shorter events, 0.0 us)
Async XLA Ops:
  0.0 3.1 %collective-permute-start = (f32[64,4096]{1,0:T(8,128)}, f32[64,4096]{1,0:T(8,128)S(1)}, u32[]{:S(2)}, u32[]{:S(2)}) collective-permute-start(f32[64,4096]{1,0:T(8,128)} %bitcast.1), channel_id=1, source_target_pairs={{0,4},{1,5},{2,6},{3,7},{4,0},{5,1},{6,2},{7,3},{8,12},{9,13},{10,... | collective-permute-start | bytes 3145736 | tf_op jit(solution)/shard_map/ppermute | solution.py:33
  5.2 7.5 %collective-permute-start.3 = (f32[8,9216]{1,0:T(8,128)S(1)}, f32[8,9216]{1,0:T(8,128)S(1)}, u32[]{:S(2)}, u32[]{:S(2)}) collective-permute-start(f32[8,9216]{1,0:T(8,128)S(1)} %get-tuple-element.43), channel_id=1, source_target_pairs={{0,16},{1,4},{2,5},{3,6},{4,1},{5,2},{6,3},{7,23},{8,24},{9,12},{1... | collective-permute-start | bytes 884744 | tf_op jit(solution)/shard_map/ppermute | solution.py:33
  8.0 7.4 %collective-permute-start.2 = (f32[8,5632]{1,0:T(8,128)S(1)}, f32[8,5632]{1,0:T(8,128)S(1)}, u32[]{:S(2)}, u32[]{:S(2)}) collective-permute-start(f32[8,5632]{1,0:T(8,128)S(1)} %get-tuple-element.38), channel_id=1, source_target_pairs={{0,8},{1,9},{2,10},{3,11},{4,12},{5,13},{6,14},{7,15},{8,0},{9,1},... | collective-permute-start | bytes 540680 | tf_op jit(solution)/shard_map/ppermute | solution.py:33
  8.0 10.5 %collective-permute-start.1 = (f32[8,5632]{1,0:T(8,128)S(1)}, f32[8,5632]{1,0:T(8,128)S(1)}, u32[]{:S(2)}, u32[]{:S(2)}) collective-permute-start(f32[8,5632]{1,0:T(8,128)S(1)} %get-tuple-element.36), channel_id=1, source_target_pairs={{0,8},{1,9},{2,10},{3,11},{4,12},{5,13},{6,14},{7,15},{8,0},{9,1},... | collective-permute-start | bytes 540680 | tf_op jit(solution)/shard_map/ppermute | solution.py:33
  18.6 8.1 %collective-permute-start.7 = (f32[32,4096]{1,0:T(8,128)S(1)}, f32[32,4096]{1,0:T(8,128)S(1)}, u32[]{:S(2)}, u32[]{:S(2)}) collective-permute-start(f32[32,4096]{1,0:T(8,128)S(1)} %get-tuple-element.58), channel_id=1, source_target_pairs={{0,4},{1,5},{2,6},{3,7},{4,0},{5,1},{6,2},{7,3},{8,12},{9,13},{10,... | collective-permute-start | bytes 1572872 | tf_op jit(solution)/shard_map/ppermute | solution.py:33
  18.7 6.4 %collective-permute-start.4 = (f32[8,4096]{1,0:T(8,128)S(1)}, f32[8,4096]{1,0:T(8,128)S(1)}, u32[]{:S(2)}, u32[]{:S(2)}) collective-permute-start(f32[8,4096]{1,0:T(8,128)S(1)} %get-tuple-element.41), channel_id=1, source_target_pairs={{0,8},{1,9},{2,10},{3,11},{4,12},{5,13},{6,14},{7,15},{8,0},{9,1},... | collective-permute-start | bytes 393224 | tf_op jit(solution)/shard_map/ppermute | solution.py:33
  19.6 7.1 %collective-permute-start.5 = (f32[8,3072]{1,0:T(8,128)S(1)}, f32[8,3072]{1,0:T(8,128)S(1)}, u32[]{:S(2)}, u32[]{:S(2)}) collective-permute-start(f32[8,3072]{1,0:T(8,128)S(1)} %get-tuple-element.48), channel_id=1, source_target_pairs={{0,8},{1,9},{2,10},{3,11},{4,12},{5,13},{6,14},{7,15},{8,0},{9,1},... | collective-permute-start | bytes 294920 | tf_op jit(solution)/shard_map/ppermute | solution.py:33
  25.2 1.6 %collective-permute-start.8 = (f32[8,4096]{1,0:T(8,128)S(1)}, f32[8,4096]{1,0:T(8,128)S(1)}, u32[]{:S(2)}, u32[]{:S(2)}) collective-permute-start(f32[8,4096]{1,0:T(8,128)S(1)} %get-tuple-element.59), channel_id=1, source_target_pairs={{0,4},{1,5},{2,6},{3,7},{4,0},{5,1},{6,2},{7,3},{8,12},{9,13},{10,... | collective-permute-start | bytes 393224 | tf_op jit(solution)/shard_map/ppermute | solution.py:33
  26.7 1.3 %collective-permute-start.6 = (f32[8,4096]{1,0:T(8,128)S(1)}, f32[8,4096]{1,0:T(8,128)S(1)}, u32[]{:S(2)}, u32[]{:S(2)}) collective-permute-start(f32[8,4096]{1,0:T(8,128)S(1)} %get-tuple-element.51), channel_id=1, source_target_pairs={{0,4},{1,5},{2,6},{3,7},{4,0},{5,1},{6,2},{7,3},{8,12},{9,13},{10,... | collective-permute-start | bytes 393224 | tf_op jit(solution)/shard_map/ppermute | solution.py:33

commit v3 on v2

--- a/solution.py
+++ b/solution.py
@@ -163,6 +163,15 @@
         jnp.concatenate([four, pltpu.roll(four, 4, 0)], axis=1),
         jnp.concatenate(low, axis=1),
     )
+
+
+def halved(v):
+    half = v.shape[1] // 2
+    return mixed(v[:, :half], pltpu.roll(v[:, half:], 4, 0))
+
+
+def unhalved(v):
+    return jnp.concatenate([v, pltpu.roll(v, 4, 0)], axis=1)
 
 
 def place():
@@ -242,9 +251,9 @@
             for i in range(count)
         ]
         part = jnp.where(
-            first, frame[8 * count : 8 * count + 8], pltpu.roll(frame[:8], 6, 0)
+            first, frame[8 * count : 8 * count + 8], pltpu.roll(frame[:8], 4, 0)
         )
-        sent[...] = jnp.concatenate([*whole, folded(part)], axis=1)
+        sent[...] = jnp.concatenate([*whole, halved(part)], axis=1)
         ends[0:half, :] = e_a
         ends[half : 2 * half, :] = e_b
 
@@ -350,23 +359,34 @@
             state[24 * kind : 24 * kind + 24, :] = jnp.concatenate([top, mid, low])
 
 
-def inner_end(half, left, right, drive, mine, theirs, keep, send, frame):
+def boundary_kernel(left, right, rows):
+    size = rows.shape[1] // 2
+    start = left.shape[1] - size
+    rows[:, :size] = left[:, start:]
+    rows[:, size:] = right[:, start:]
+
+
+def inner_end(half, left, right, beyond, drive, mine, theirs, keep, send, frame):
     core, chip = place()
     first = core == 0
 
     @pl.when(chip > 0)
     def _():
         count = half // 8 - 2
-        mid = left.shape[1] * 4 // (4 * count + 3)
+        mid = left.shape[1] * 2 // (2 * count + 1)
         parts = left[...], right[...]
 
         def across(begin, end, change=same):
             return jnp.concatenate([change(p[:, begin:end]) for p in parts], axis=1)
 
         whole = [across(i * mid, i * mid + mid) for i in range(count)]
-        part = across(count * mid, left.shape[1], unfolded)
+        near = across(count * mid, left.shape[1], unhalved)
+        far = [beyond[:, : mid // 2], beyond[:, mid // 2 :]]
+        far = jnp.concatenate([unhalved(v) for v in far], axis=1)
+        top, low = picked(first, near, far)
+        part = mixed(top, pltpu.roll(low, 4, 0))
         upper = [*whole, part]
-        lower = [pltpu.roll(part, 2, 0), *whole]
+        lower = [part, *whole]
         rows = jnp.concatenate([jnp.where(first, u, v) for u, v in zip(upper, lower)])
         frame[...] = rows
         current = pltpu.roll(jnp.concatenate([rows, rows[:8]]), CUT, 0)
@@ -637,7 +657,7 @@
         name="load",
     )(starts, drive)
     mid = width // 2
-    packed = mid * (half // 8 - 2) + mid * 3 // 4
+    packed = mid * (half // 8 - 2) + mid // 2
     sent_l, ends_l = compute(
         functools.partial(inner_kernel, half, 0),
         [(8, packed), (height, mid)],
@@ -666,6 +686,8 @@
         (own, other, after(held, delta_other), got),
     )
     here_3 = routed(sent_3, stage_swap(0))
+    (rows_1,) = compute(boundary_kernel, [(8, mid)], (here_l, after(here_r, sent_3)))
+    beyond = routed(rows_1, partner)
     (state_3,) = compute(
         functools.partial(outer_state_kernel, half),
         [(3 * 24, width)],
@@ -674,7 +696,7 @@
     near_keep, near_send, frame = compute(
         functools.partial(inner_end, half),
         [(half - 16, width), (half - 16, width), (half - 8, width)],
-        (here_l, here_r, held, delta_own, after(delta_other, state_3)),
+        (here_l, here_r, beyond, held, delta_own, after(delta_other, state_3)),
     )
     keep_1, send_1 = compute(
         functools.partial(gather_kernel, half),

time: 28.3 us -> 28.8 us (1.018)
  waiting for transfers between devices: 11.7 us -> 12.2 us
    ppermute x9 -> x10, waiting for transfers between devices: 11.7 us -> 12.2 us  [routed(): return lax.ppermute(block, AXES, pairs)]
    ppermute x9 -> x10, starting transfers between devices: 7.49 us -> 7.57 us  [routed(): return lax.ppermute(block, AXES, pairs)]
    pallas_call x10 -> x11, Pallas kernels: 5.15 us -> 5.15 us  [compute(): pl.pallas_call(kernel, out_shape=shapes, in_specs=[vmem] * len(args), out...]
  transfers between devices with their start and end apart: 9 -> 10, of which waited for: 6 -> 7; matrix products, arithmetic and copies ran while one was open for 0% -> 0% of each run, Pallas kernels for 23% -> 23%
where the time goes in v3:
time: 28.8 us; the launch traced here: 28.7 us
  waiting for transfers between devices  12.2 us (42%)
  Pallas kernels  8.83 us (31%)
  starting transfers between devices  7.57 us (26%)
    ppermute x10, waiting for transfers between devices, routed(): return lax.ppermute(block, AXES, pairs)  12.2 us
    ppermute x10, starting transfers between devices, routed(): return lax.ppermute(block, AXES, pairs)  7.57 us
    pallas_call x11, Pallas kernels, compute(): pl.pallas_call(kernel, out_shape=shapes, in_specs=[vmem] * len(args), out...  5.15 us
    pallas_call x1, Pallas kernels, two_chips(): pl.pallas_call(functools.partial(load_kernel, half), out_shape=[jax.Shape...  2.6 us
    pallas_call x2, Pallas kernels, written(): pl.pallas_call(functools.partial(write_kernel, half, into is not None), o...  1.08 us
  transfers between devices with their start and end apart: 10, of which 7 were waited for; matrix products, arithmetic and copies ran while one was open for 0% of the time, Pallas kernels for 23%

profile of v3, /device:TPU:0, one launch (start us, length us, event | category | flops | bytes accessed | tf_op | source)
XLA Modules:
  0.0 28.7 jit_solution(18395883666964154953)
XLA Ops:
  0.0 0.5 %collective-permute-start = (f32[64,4096]{1,0:T(8,128)}, f32[64,4096]{1,0:T(8,128)S(1)}, u32[]{:S(2)}, u32[]{:S(2)}) collective-permute-start(f32[64,4096]{1,0:T(8,128)} %bitcast.1), channel_id=1, source_target_pairs={{0,4},{1,5},{2,6},{3,7},{4,0},{5,1},{6,2},{7,3},{8,12},{9,13},{10,... | collective-permute-start | bytes 3145736 | tf_op jit(solution)/shard_map/ppermute | solution.py:33
  0.5 2.6 %load.1 = (f32[64,4096]{1,0:T(8,128)S(1)}, f32[64,4096]{1,0:T(8,128)S(1)}, f32[64,4096]{1,0:T(8,128)S(1)}) custom-call(f32[1,64,4096]{2,1,0:T(8,128)} %starts.1, f32[64,4096]{1,0:T(8,128)} %drive.1), custom_call_target="tpu_custom_call" | custom-call | flops 5898240 | bytes 4194304 | tf_op jit(solution)/shard_map/load/pallas_call | solution.py:645
  3.1 0.0 collective-permute-done.other
  3.1 1.0 %shard_map.28 = (f32[8,5120]{1,0:T(8,128)S(1)}, f32[64,2048]{1,0:T(8,128)S(1)}) custom-call(f32[64,4096]{1,0:T(8,128)S(1)} %get-tuple-element.34.own, f32[64,4096]{1,0:T(8,128)S(1)} %collective-permute-done.other, f32[64,4096]{1,0:T(8,128)S(1)} %get-tuple-element.43.drive, f32[64,4096]{1,0:T(8,128)S(1)} %get-tuple-element.38.mine), custom_call_target="tpu_custom_call" | custom-call | tf_op jit(solution)/shard_map/pallas_call | solution.py:90
  4.1 1.1 %shard_map.29 = (f32[8,5120]{1,0:T(8,128)S(1)}, f32[64,2048]{1,0:T(8,128)S(1)}, f32[8,9216]{1,0:T(8,128)S(1)}) custom-call(f32[64,4096]{1,0:T(8,128)S(1)} %get-tuple-element.34.own, f32[64,4096]{1,0:T(8,128)S(1)} %collective-permute-done.other, f32[64,4096]{1,0:T(8,128)S(1)} %get-tuple-element.43.drive, f32[64,4096]{1,0:T(8,128)S(1)} %get-tuple-element.38.mine), custom_call_target="tpu_custom_call" | custom-call | tf_op jit(solution)/shard_map/pallas_call | solution.py:90
  5.2 2.8 %collective-permute-start.3 = (f32[8,9216]{1,0:T(8,128)S(1)}, f32[8,9216]{1,0:T(8,128)S(1)}, u32[]{:S(2)}, u32[]{:S(2)}) collective-permute-start(f32[8,9216]{1,0:T(8,128)S(1)} %get-tuple-element.44), channel_id=1, source_target_pairs={{0,16},{1,4},{2,5},{3,6},{4,1},{5,2},{6,3},{7,23},{8,24},{9,12},{1... | collective-permute-start | bytes 884744 | tf_op jit(solution)/shard_map/ppermute | solution.py:33
  8.0 0.0 collective-permute-start.2
  8.0 2.0 %collective-permute-start.1 = (f32[8,5120]{1,0:T(8,128)S(1)}, f32[8,5120]{1,0:T(8,128)S(1)}, u32[]{:S(2)}, u32[]{:S(2)}) collective-permute-start(f32[8,5120]{1,0:T(8,128)S(1)} %get-tuple-element.37), channel_id=1, source_target_pairs={{0,8},{1,9},{2,10},{3,11},{4,12},{5,13},{6,14},{7,15},{8,0},{9,1},... | collective-permute-start | bytes 491528 | tf_op jit(solution)/shard_map/ppermute | solution.py:33
  10.0 1.4 %shard_map.30 = (f32[8,4096]{1,0:T(8,128)S(1)}, f32[32,4096]{1,0:T(8,128)S(1)}, f32[40,4096]{1,0:T(8,128)S(1)}) custom-call(f32[64,4096]{1,0:T(8,128)S(1)} %get-tuple-element.34.own, f32[64,4096]{1,0:T(8,128)S(1)} %collective-permute-done.other, f32[64,4096]{1,0:T(8,128)S(1)} %get-tuple-element.43.drive), custom_call_target="tpu_custom_call" | custom-call | tf_op jit(solution)/shard_map/pallas_call | solution.py:90
  11.4 1.3 %collective-permute-done.3.got = f32[8,9216]{1,0:T(8,128)S(1)} collective-permute-done((f32[8,9216]{1,0:T(8,128)S(1)}, f32[8,9216]{1,0:T(8,128)S(1)}, u32[]{:S(2)}, u32[]{:S(2)}) %collective-permute-start.3) | collective-permute-done | bytes 294944 | tf_op jit(solution)/shard_map/ppermute | solution.py:33
  12.7 1.5 %shard_map.32 = (f32[8,3072]{1,0:T(8,128)S(1)}, f32[32,4096]{1,0:T(8,128)S(1)}) custom-call(f32[64,4096]{1,0:T(8,128)S(1)} %get-tuple-element.34.own, f32[64,4096]{1,0:T(8,128)S(1)} %collective-permute-done.other, f32[64,4096]{1,0:T(8,128)S(1)} %get-tuple-element.43.drive, f32[8,9216]{1,0:T(8,128)S(1)} %collective-permute-done.3.got), custom_call_target="tpu_custom_call" | custom-call | tf_op jit(solution)/shard_map/pallas_call | solution.py:90
  14.2 0.8 %collective-permute-done.2.right = f32[8,5120]{1,0:T(8,128)S(1)} collective-permute-done((f32[8,5120]{1,0:T(8,128)S(1)}, f32[8,5120]{1,0:T(8,128)S(1)}, u32[]{:S(2)}, u32[]{:S(2)}) %collective-permute-start.2) | collective-permute-done | bytes 163872 | tf_op jit(solution)/shard_map/ppermute | solution.py:33
  15.0 2.7 %collective-permute-done.1.left = f32[8,5120]{1,0:T(8,128)S(1)} collective-permute-done((f32[8,5120]{1,0:T(8,128)S(1)}, f32[8,5120]{1,0:T(8,128)S(1)}, u32[]{:S(2)}, u32[]{:S(2)}) %collective-permute-start.1) | collective-permute-done | bytes 163872 | tf_op jit(solution)/shard_map/ppermute | solution.py:33
  17.8 0.0 collective-permute-start.4
  17.8 1.2 %collective-permute-done.4.beyond = f32[8,2048]{1,0:T(8,128)S(1)} collective-permute-done((f32[8,2048]{1,0:T(8,128)S(1)}, f32[8,2048]{1,0:T(8,128)S(1)}, u32[]{:S(2)}, u32[]{:S(2)}) %collective-permute-start.4) | collective-permute-done | bytes 65568 | tf_op jit(solution)/shard_map/ppermute | solution.py:33
  19.0 0.2 shard_map.38
  19.2 0.2 collective-permute-start.8
  19.4 0.9 %collective-permute-start.5 = (f32[8,4096]{1,0:T(8,128)S(1)}, f32[8,4096]{1,0:T(8,128)S(1)}, u32[]{:S(2)}, u32[]{:S(2)}) collective-permute-start(f32[8,4096]{1,0:T(8,128)S(1)} %get-tuple-element.41), channel_id=1, source_target_pairs={{0,8},{1,9},{2,10},{3,11},{4,12},{5,13},{6,14},{7,15},{8,0},{9,1},... | collective-permute-start | bytes 393224 | tf_op jit(solution)/shard_map/ppermute | solution.py:33
  20.3 1.2 %collective-permute-start.6 = (f32[8,3072]{1,0:T(8,128)S(1)}, f32[8,3072]{1,0:T(8,128)S(1)}, u32[]{:S(2)}, u32[]{:S(2)}) collective-permute-start(f32[8,3072]{1,0:T(8,128)S(1)} %get-tuple-element.45), channel_id=1, source_target_pairs={{0,8},{1,9},{2,10},{3,11},{4,12},{5,13},{6,14},{7,15},{8,0},{9,1},... | collective-permute-start | bytes 294920 | tf_op jit(solution)/shard_map/ppermute | solution.py:33
  21.4 4.3 %collective-permute-done.5.middle = f32[8,4096]{1,0:T(8,128)S(1)} collective-permute-done((f32[8,4096]{1,0:T(8,128)S(1)}, f32[8,4096]{1,0:T(8,128)S(1)}, u32[]{:S(2)}, u32[]{:S(2)}) %collective-permute-start.5) | collective-permute-done | bytes 131104 | tf_op jit(solution)/shard_map/ppermute | solution.py:33
  25.8 0.0 collective-permute-start.9
  25.8 1.5 %collective-permute-done.6.outer = f32[8,3072]{1,0:T(8,128)S(1)} collective-permute-done((f32[8,3072]{1,0:T(8,128)S(1)}, f32[8,3072]{1,0:T(8,128)S(1)}, u32[]{:S(2)}, u32[]{:S(2)}) %collective-permute-start.6) | collective-permute-done | bytes 98336 | tf_op jit(solution)/shard_map/ppermute | solution.py:33
  27.3 0.0 collective-permute-start.7
  27.3 0.0 collective-permute-done.9.refs_3_
  27.3 0.0 collective-permute-done.8.refs_1_
  27.3 1.0 %shard_map.39.refs_1_ = f32[1,64,4096]{2,1,0:T(8,128)} custom-call(f32[32,4096]{1,0:T(8,128)S(1)} %get-tuple-element.59.refs_0_, f32[32,4096]{1,0:T(8,128)S(1)} %collective-permute-done.8.refs_1_, f32[8,4096]{1,0:T(8,128)S(1)} %get-tuple-element.51.refs_2_, f32[8,4096]{1,0:T(8,128)S(1)} %collective-permute-done.9.refs_3_, ...), custom_call_target="tpu_custom_call" | custom-call | tf_op jit(solution)/shard_map/pallas_call | solution.py:542
  28.3 0.3 %collective-permute-done.7.refs_0_ = f32[8,4096]{1,0:T(8,128)S(1)} collective-permute-done((f32[8,4096]{1,0:T(8,128)S(1)}, f32[8,4096]{1,0:T(8,128)S(1)}, u32[]{:S(2)}, u32[]{:S(2)}) %collective-permute-start.7) | collective-permute-done | bytes 131104 | tf_op jit(solution)/shard_map/ppermute | solution.py:33
  28.6 0.1 shard_map.40
  (6 shorter events, 0.1 us)
Async XLA Ops:
  0.0 3.1 %collective-permute-start = (f32[64,4096]{1,0:T(8,128)}, f32[64,4096]{1,0:T(8,128)S(1)}, u32[]{:S(2)}, u32[]{:S(2)}) collective-permute-start(f32[64,4096]{1,0:T(8,128)} %bitcast.1), channel_id=1, source_target_pairs={{0,4},{1,5},{2,6},{3,7},{4,0},{5,1},{6,2},{7,3},{8,12},{9,13},{10,... | collective-permute-start | bytes 3145736 | tf_op jit(solution)/shard_map/ppermute | solution.py:33
  5.2 7.5 %collective-permute-start.3 = (f32[8,9216]{1,0:T(8,128)S(1)}, f32[8,9216]{1,0:T(8,128)S(1)}, u32[]{:S(2)}, u32[]{:S(2)}) collective-permute-start(f32[8,9216]{1,0:T(8,128)S(1)} %get-tuple-element.44), channel_id=1, source_target_pairs={{0,16},{1,4},{2,5},{3,6},{4,1},{5,2},{6,3},{7,23},{8,24},{9,12},{1... | collective-permute-start | bytes 884744 | tf_op jit(solution)/shard_map/ppermute | solution.py:33
  8.0 7.1 %collective-permute-start.2 = (f32[8,5120]{1,0:T(8,128)S(1)}, f32[8,5120]{1,0:T(8,128)S(1)}, u32[]{:S(2)}, u32[]{:S(2)}) collective-permute-start(f32[8,5120]{1,0:T(8,128)S(1)} %get-tuple-element.39), channel_id=1, source_target_pairs={{0,8},{1,9},{2,10},{3,11},{4,12},{5,13},{6,14},{7,15},{8,0},{9,1},... | collective-permute-start | bytes 491528 | tf_op jit(solution)/shard_map/ppermute | solution.py:33
  8.0 9.8 %collective-permute-start.1 = (f32[8,5120]{1,0:T(8,128)S(1)}, f32[8,5120]{1,0:T(8,128)S(1)}, u32[]{:S(2)}, u32[]{:S(2)}) collective-permute-start(f32[8,5120]{1,0:T(8,128)S(1)} %get-tuple-element.37), channel_id=1, source_target_pairs={{0,8},{1,9},{2,10},{3,11},{4,12},{5,13},{6,14},{7,15},{8,0},{9,1},... | collective-permute-start | bytes 491528 | tf_op jit(solution)/shard_map/ppermute | solution.py:33
  17.8 1.3 %collective-permute-start.4 = (f32[8,2048]{1,0:T(8,128)S(1)}, f32[8,2048]{1,0:T(8,128)S(1)}, u32[]{:S(2)}, u32[]{:S(2)}) collective-permute-start(f32[8,2048]{1,0:T(8,128)S(1)} %shard_map.33), channel_id=1, source_target_pairs={{0,4},{1,5},{2,6},{3,7},{4,0},{5,1},{6,2},{7,3},{8,12},{9,13},{10,... | collective-permute-start | bytes 196616 | tf_op jit(solution)/shard_map/ppermute | solution.py:33
  19.2 8.1 %collective-permute-start.8 = (f32[32,4096]{1,0:T(8,128)S(1)}, f32[32,4096]{1,0:T(8,128)S(1)}, u32[]{:S(2)}, u32[]{:S(2)}) collective-permute-start(f32[32,4096]{1,0:T(8,128)S(1)} %get-tuple-element.60), channel_id=1, source_target_pairs={{0,4},{1,5},{2,6},{3,7},{4,0},{5,1},{6,2},{7,3},{8,12},{9,13},{10,... | collective-permute-start | bytes 1572872 | tf_op jit(solution)/shard_map/ppermute | solution.py:33
  19.4 6.4 %collective-permute-start.5 = (f32[8,4096]{1,0:T(8,128)S(1)}, f32[8,4096]{1,0:T(8,128)S(1)}, u32[]{:S(2)}, u32[]{:S(2)}) collective-permute-start(f32[8,4096]{1,0:T(8,128)S(1)} %get-tuple-element.41), channel_id=1, source_target_pairs={{0,8},{1,9},{2,10},{3,11},{4,12},{5,13},{6,14},{7,15},{8,0},{9,1},... | collective-permute-start | bytes 393224 | tf_op jit(solution)/shard_map/ppermute | solution.py:33
  20.3 7.0 %collective-permute-start.6 = (f32[8,3072]{1,0:T(8,128)S(1)}, f32[8,3072]{1,0:T(8,128)S(1)}, u32[]{:S(2)}, u32[]{:S(2)}) collective-permute-start(f32[8,3072]{1,0:T(8,128)S(1)} %get-tuple-element.45), channel_id=1, source_target_pairs={{0,8},{1,9},{2,10},{3,11},{4,12},{5,13},{6,14},{7,15},{8,0},{9,1},... | collective-permute-start | bytes 294920 | tf_op jit(solution)/shard_map/ppermute | solution.py:33
  25.8 1.5 %collective-permute-start.9 = (f32[8,4096]{1,0:T(8,128)S(1)}, f32[8,4096]{1,0:T(8,128)S(1)}, u32[]{:S(2)}, u32[]{:S(2)}) collective-permute-start(f32[8,4096]{1,0:T(8,128)S(1)} %get-tuple-element.61), channel_id=1, source_target_pairs={{0,4},{1,5},{2,6},{3,7},{4,0},{5,1},{6,2},{7,3},{8,12},{9,13},{10,... | collective-permute-start | bytes 393224 | tf_op jit(solution)/shard_map/ppermute | solution.py:33
  27.3 1.3 %collective-permute-start.7 = (f32[8,4096]{1,0:T(8,128)S(1)}, f32[8,4096]{1,0:T(8,128)S(1)}, u32[]{:S(2)}, u32[]{:S(2)}) collective-permute-start(f32[8,4096]{1,0:T(8,128)S(1)} %get-tuple-element.53), channel_id=1, source_target_pairs={{0,4},{1,5},{2,6},{3,7},{4,0},{5,1},{6,2},{7,3},{8,12},{9,13},{10,... | collective-permute-start | bytes 393224 | tf_op jit(solution)/shard_map/ppermute | solution.py:33

commit v4 on v3

--- a/solution.py
+++ b/solution.py
@@ -27,9 +27,11 @@
     for g in range(groups):
         for t in range(slices):
             for r in range(rows):
-                to_g, to_t, to_r = route(g, t, r)
-                source = (g * slices + t) * rows + r
-                pairs.append((source, (to_g * slices + to_t) * rows + to_r))
+                target = route(g, t, r)
+                if target is not None:
+                    to_g, to_t, to_r = target
+                    source = (g * slices + t) * rows + r
+                    pairs.append((source, (to_g * slices + to_t) * rows + to_r))
     return lax.ppermute(block, AXES, pairs)
 
 
@@ -56,6 +58,13 @@
         if chip == stage + 1:
             return g, t - 2, r
         return g, t, r
+
+    return route
+
+
+def stage_send(stage):
+    def route(g, t, r):
+        return (g, t + 2, r) if t // 2 == stage else None
 
     return route
 
@@ -264,7 +273,7 @@
         edge[...] = jnp.concatenate([folded(v) for v in fields], axis=1)
 
 
-def middle_kernel(half, own, other, drive, sent, ends, delta):
+def middle_kernel(half, own, other, drive, sent, ends):
     core, chip = place()
     first = core == 0
 
@@ -278,25 +287,20 @@
         ends[0:16, :] = e_a
         ends[16:32, :] = e_b
 
-    @pl.when(chip > 0)
-    def _():
-        rows = receiver_rows(half, core)
-        fine, coarse = start_of(own[rows, :], drive[rows, :])
-        delta[...] = fine - coarse
-
 
 def receiver_rows(half, core):
     return pl.ds(pl.multiple_of((half - WIDE) * core, 8), half + WIDE)
 
 
-def state_kernel(half, other, drive, theirs):
+def state_kernel(half, own, other, drive, mine, theirs):
     core, chip = place()
 
     @pl.when(chip > 0)
     def _():
         rows = receiver_rows(half, core)
-        fine, coarse = start_of(other[rows, :], drive[rows, :])
-        theirs[...] = fine - coarse
+        for ref, delta in ((own, mine), (other, theirs)):
+            fine, coarse = start_of(ref[rows, :], drive[rows, :])
+            delta[...] = fine - coarse
 
 
 def outer_window(half, own, other, drive, got):
@@ -671,14 +675,16 @@
     )
     here_r = routed(sent_r, stage_swap(0))
     got = routed(edge, outward(groups, rows))
-    sent_2, ends_2, delta_own = compute(
+    sent_2, ends_2 = compute(
         functools.partial(middle_kernel, half),
-        [(8, width), (32, width), (half + WIDE, width)],
+        [(8, width), (32, width)],
         (own, other, after(held, sent_r)),
     )
-    here_2 = routed(sent_2, stage_swap(0))
-    (delta_other,) = compute(
-        functools.partial(state_kernel, half), [(half + WIDE, width)], (other, after(held, sent_2))
+    here_2 = routed(sent_2, stage_send(0))
+    delta_own, delta_other = compute(
+        functools.partial(state_kernel, half),
+        [(half + WIDE, width)] * 2,
+        (own, other, after(held, sent_2)),
     )
     sent_3, ends_3 = compute(
         functools.partial(outer_kernel, half),

time: 28.8 us -> 30.2 us (1.049)
  the two profiles are of different devices: /device:TPU:0 before, /device:TPU:3 now
where the time goes in v4:
time: 30.2 us; the launch traced here: 30 us
  starting transfers between devices  12 us (40%)
  Pallas kernels  9.44 us (31%)
  waiting for transfers between devices  8.54 us (28%)
    ppermute x10, starting transfers between devices, routed(): return lax.ppermute(block, AXES, pairs)  12 us
    ppermute x10, waiting for transfers between devices, routed(): return lax.ppermute(block, AXES, pairs)  8.54 us
    pallas_call x11, Pallas kernels, compute(): pl.pallas_call(kernel, out_shape=shapes, in_specs=[vmem] * len(args), out...  6.2 us
    pallas_call x2, Pallas kernels, written(): pl.pallas_call(functools.partial(write_kernel, half, into is not None), o...  1.69 us
    pallas_call x1, Pallas kernels, two_chips(): pl.pallas_call(functools.partial(load_kernel, half), out_shape=[jax.Shape...  1.55 us
  transfers between devices with their start and end apart: 10, of which 5 were waited for; matrix products, arithmetic and copies ran while one was open for 0% of the time, Pallas kernels for 26%

profile of v4, /device:TPU:3, one launch (start us, length us, event | category | flops | bytes accessed | tf_op | source)
XLA Modules:
  0.0 30.0 jit_solution(14035549890975682253)
XLA Ops:
  0.0 0.7 %collective-permute-start = (f32[64,4096]{1,0:T(8,128)}, f32[64,4096]{1,0:T(8,128)S(1)}, u32[]{:S(2)}, u32[]{:S(2)}) collective-permute-start(f32[64,4096]{1,0:T(8,128)} %bitcast.1), channel_id=1, source_target_pairs={{0,4},{1,5},{2,6},{3,7},{4,0},{5,1},{6,2},{7,3},{8,12},{9,13},{10,... | collective-permute-start | bytes 3145736 | tf_op jit(solution)/shard_map/ppermute | solution.py:35
  0.7 1.5 %load.1 = (f32[64,4096]{1,0:T(8,128)S(1)}, f32[64,4096]{1,0:T(8,128)S(1)}, f32[64,4096]{1,0:T(8,128)S(1)}) custom-call(f32[1,64,4096]{2,1,0:T(8,128)} %starts.1, f32[64,4096]{1,0:T(8,128)} %drive.1), custom_call_target="tpu_custom_call" | custom-call | flops 5898240 | bytes 4194304 | tf_op jit(solution)/shard_map/load/pallas_call | solution.py:649
  2.2 0.9 %collective-permute-done.other = f32[64,4096]{1,0:T(8,128)S(1)} collective-permute-done((f32[64,4096]{1,0:T(8,128)}, f32[64,4096]{1,0:T(8,128)S(1)}, u32[]{:S(2)}, u32[]{:S(2)}) %collective-permute-start) | collective-permute-done | bytes 1048608 | tf_op jit(solution)/shard_map/ppermute | solution.py:35
  3.2 0.1 shard_map.29
  3.3 1.6 %collective-permute-start.3 = (f32[8,9216]{1,0:T(8,128)S(1)}, f32[8,9216]{1,0:T(8,128)S(1)}, u32[]{:S(2)}, u32[]{:S(2)}) collective-permute-start(f32[8,9216]{1,0:T(8,128)S(1)} %get-tuple-element.46), channel_id=1, source_target_pairs={{0,16},{1,4},{2,5},{3,6},{4,1},{5,2},{6,3},{7,23},{8,24},{9,12},{1... | collective-permute-start | bytes 884744 | tf_op jit(solution)/shard_map/ppermute | solution.py:35
  4.9 2.2 %collective-permute-start.2 = (f32[8,5120]{1,0:T(8,128)S(1)}, f32[8,5120]{1,0:T(8,128)S(1)}, u32[]{:S(2)}, u32[]{:S(2)}) collective-permute-start(f32[8,5120]{1,0:T(8,128)S(1)} %get-tuple-element.40), channel_id=1, source_target_pairs={{0,8},{1,9},{2,10},{3,11},{4,12},{5,13},{6,14},{7,15},{8,0},{9,1},... | collective-permute-start | bytes 491528 | tf_op jit(solution)/shard_map/ppermute | solution.py:35
  7.1 0.0 collective-permute-start.1
  7.1 2.9 %shard_map.31 = (f32[40,4096]{1,0:T(8,128)S(1)}, f32[40,4096]{1,0:T(8,128)S(1)}) custom-call(f32[64,4096]{1,0:T(8,128)S(1)} %get-tuple-element.35.own, f32[64,4096]{1,0:T(8,128)S(1)} %collective-permute-done.other, f32[64,4096]{1,0:T(8,128)S(1)} %get-tuple-element.45.drive), custom_call_target="tpu_custom_call" | custom-call | tf_op jit(solution)/shard_map/pallas_call | solution.py:99
  10.0 0.0 collective-permute-done.3.got
  10.0 0.7 %shard_map.32 = (f32[8,3072]{1,0:T(8,128)S(1)}, f32[32,4096]{1,0:T(8,128)S(1)}) custom-call(f32[64,4096]{1,0:T(8,128)S(1)} %get-tuple-element.35.own, f32[64,4096]{1,0:T(8,128)S(1)} %collective-permute-done.other, f32[64,4096]{1,0:T(8,128)S(1)} %get-tuple-element.45.drive, f32[8,9216]{1,0:T(8,128)S(1)} %collective-permute-done.3.got), custom_call_target="tpu_custom_call" | custom-call | tf_op jit(solution)/shard_map/pallas_call | solution.py:99
  10.7 0.6 %collective-permute-done.2.right = f32[8,5120]{1,0:T(8,128)S(1)} collective-permute-done((f32[8,5120]{1,0:T(8,128)S(1)}, f32[8,5120]{1,0:T(8,128)S(1)}, u32[]{:S(2)}, u32[]{:S(2)}) %collective-permute-start.2) | collective-permute-done | bytes 163872 | tf_op jit(solution)/shard_map/ppermute | solution.py:35
  11.3 3.5 %collective-permute-done.1.left = f32[8,5120]{1,0:T(8,128)S(1)} collective-permute-done((f32[8,5120]{1,0:T(8,128)S(1)}, f32[8,5120]{1,0:T(8,128)S(1)}, u32[]{:S(2)}, u32[]{:S(2)}) %collective-permute-start.1) | collective-permute-done | bytes 163872 | tf_op jit(solution)/shard_map/ppermute | solution.py:35
  14.8 0.9 %collective-permute-start.4 = (f32[8,2048]{1,0:T(8,128)S(1)}, f32[8,2048]{1,0:T(8,128)S(1)}, u32[]{:S(2)}, u32[]{:S(2)}) collective-permute-start(f32[8,2048]{1,0:T(8,128)S(1)} %shard_map.33), channel_id=1, source_target_pairs={{0,4},{1,5},{2,6},{3,7},{4,0},{5,1},{6,2},{7,3},{8,12},{9,13},{10,... | collective-permute-start | bytes 196616 | tf_op jit(solution)/shard_map/ppermute | solution.py:35
  15.8 0.7 %shard_map.34.state = f32[72,4096]{1,0:T(8,128)S(1)} custom-call(f32[64,4096]{1,0:T(8,128)S(1)} %get-tuple-element.35.own, f32[64,4096]{1,0:T(8,128)S(1)} %collective-permute-done.other, f32[64,4096]{1,0:T(8,128)S(1)} %get-tuple-element.45.drive, f32[8,9216]{1,0:T(8,128)S(1)} %collective-permute-done.3.got, f32[40,4096]{1,0:T(8,128)S(1)} %get-tuple-element.49.mine, ...), custom_call_target="tpu_custom_call" | custom-call | tf_op jit(solution)/shard_map/pallas_call | solution.py:99
  16.5 0.2 collective-permute-done.4.beyond
  16.7 0.7 %shard_map.35 = (f32[16,4096]{1,0:T(8,128)S(1)}, f32[16,4096]{1,0:T(8,128)S(1)}, f32[24,4096]{1,0:T(8,128)S(1)}) custom-call(f32[8,5120]{1,0:T(8,128)S(1)} %collective-permute-done.1.left, f32[8,5120]{1,0:T(8,128)S(1)} %collective-permute-done.2.right, f32[8,2048]{1,0:T(8,128)S(1)} %collective-permute-done.4.beyond, f32[64,4096]{1,0:T(8,128)S(1)} %get-tuple-element.45.drive, ...), custom_call_target="tpu_custom_call" | custom-call | tf_op jit(solution)/shard_map/pallas_call | solution.py:99
  17.4 0.1 shard_map.38
  17.4 0.4 %collective-permute-start.8 = (f32[32,4096]{1,0:T(8,128)S(1)}, f32[32,4096]{1,0:T(8,128)S(1)}, u32[]{:S(2)}, u32[]{:S(2)}) collective-permute-start(f32[32,4096]{1,0:T(8,128)S(1)} %get-tuple-element.62), channel_id=1, source_target_pairs={{0,4},{1,5},{2,6},{3,7},{4,0},{5,1},{6,2},{7,3},{8,12},{9,13},{10,... | collective-permute-start | bytes 1572872 | tf_op jit(solution)/shard_map/ppermute | solution.py:35
  17.8 1.3 %collective-permute-start.5 = (f32[8,4096]{1,0:T(8,128)S(1)}, f32[8,4096]{1,0:T(8,128)S(1)}, u32[]{:S(2)}, u32[]{:S(2)}) collective-permute-start(f32[8,4096]{1,0:T(8,128)S(1)} %get-tuple-element.42), channel_id=1, source_target_pairs={{0,8},{1,9},{2,10},{3,11},{4,12},{5,13},{6,14},{7,15},{16,24},{17,... | collective-permute-start | bytes 393224 | tf_op jit(solution)/shard_map/ppermute | solution.py:35
  19.1 2.2 %collective-permute-start.6 = (f32[8,3072]{1,0:T(8,128)S(1)}, f32[8,3072]{1,0:T(8,128)S(1)}, u32[]{:S(2)}, u32[]{:S(2)}) collective-permute-start(f32[8,3072]{1,0:T(8,128)S(1)} %get-tuple-element.47), channel_id=1, source_target_pairs={{0,8},{1,9},{2,10},{3,11},{4,12},{5,13},{6,14},{7,15},{8,0},{9,1},... | collective-permute-start | bytes 294920 | tf_op jit(solution)/shard_map/ppermute | solution.py:35
  21.3 3.3 %collective-permute-done.5.middle = f32[8,4096]{1,0:T(8,128)S(1)} collective-permute-done((f32[8,4096]{1,0:T(8,128)S(1)}, f32[8,4096]{1,0:T(8,128)S(1)}, u32[]{:S(2)}, u32[]{:S(2)}) %collective-permute-start.5) | collective-permute-done | bytes 131104 | tf_op jit(solution)/shard_map/ppermute | solution.py:35
  24.6 0.5 %shard_map.36 = (f32[8,4096]{1,0:T(8,128)S(1)}, f32[8,4096]{1,0:T(8,128)S(1)}) custom-call(f32[24,4096]{1,0:T(8,128)S(1)} %get-tuple-element.52.inner, f32[8,4096]{1,0:T(8,128)S(1)} %collective-permute-done.5.middle, f32[64,4096]{1,0:T(8,128)S(1)} %get-tuple-element.45.drive, f32[40,4096]{1,0:T(8,128)S(1)} %get-tuple-element.49.mine, ...), custom_call_target="tpu_custom_call" | custom-call | tf_op jit(solution)/shard_map/pallas_call | solution.py:99
  25.1 1.7 %collective-permute-start.9 = (f32[8,4096]{1,0:T(8,128)S(1)}, f32[8,4096]{1,0:T(8,128)S(1)}, u32[]{:S(2)}, u32[]{:S(2)}) collective-permute-start(f32[8,4096]{1,0:T(8,128)S(1)} %get-tuple-element.63), channel_id=1, source_target_pairs={{0,4},{1,5},{2,6},{3,7},{4,0},{5,1},{6,2},{7,3},{8,12},{9,13},{10,... | collective-permute-start | bytes 393224 | tf_op jit(solution)/shard_map/ppermute | solution.py:35
  26.8 0.0 collective-permute-done.6.outer
  26.8 0.5 %shard_map.37 = (f32[8,4096]{1,0:T(8,128)S(1)}, f32[8,4096]{1,0:T(8,128)S(1)}) custom-call(f32[24,4096]{1,0:T(8,128)S(1)} %get-tuple-element.52.inner, f32[8,4096]{1,0:T(8,128)S(1)} %collective-permute-done.5.middle, f32[8,3072]{1,0:T(8,128)S(1)} %collective-permute-done.6.outer, f32[72,4096]{1,0:T(8,128)S(1)} %shard_map.34.state), custom_call_target="tpu_custom_call" | custom-call | tf_op jit(solution)/shard_map/pallas_call | solution.py:99
  27.4 1.0 %collective-permute-start.7 = (f32[8,4096]{1,0:T(8,128)S(1)}, f32[8,4096]{1,0:T(8,128)S(1)}, u32[]{:S(2)}, u32[]{:S(2)}) collective-permute-start(f32[8,4096]{1,0:T(8,128)S(1)} %get-tuple-element.55), channel_id=1, source_target_pairs={{0,4},{1,5},{2,6},{3,7},{4,0},{5,1},{6,2},{7,3},{8,12},{9,13},{10,... | collective-permute-start | bytes 393224 | tf_op jit(solution)/shard_map/ppermute | solution.py:35
  28.3 0.0 collective-permute-done.9.refs_3_
  28.3 0.0 collective-permute-done.8.refs_1_
  28.3 1.0 %shard_map.39.refs_1_ = f32[1,64,4096]{2,1,0:T(8,128)} custom-call(f32[32,4096]{1,0:T(8,128)S(1)} %get-tuple-element.61.refs_0_, f32[32,4096]{1,0:T(8,128)S(1)} %collective-permute-done.8.refs_1_, f32[8,4096]{1,0:T(8,128)S(1)} %get-tuple-element.53.refs_2_, f32[8,4096]{1,0:T(8,128)S(1)} %collective-permute-done.9.refs_3_, ...), custom_call_target="tpu_custom_call" | custom-call | tf_op jit(solution)/shard_map/pallas_call | solution.py:546
  29.3 0.0 collective-permute-done.7.refs_0_
  29.3 0.7 %shard_map.40 = f32[1,64,4096]{2,1,0:T(8,128)} custom-call(f32[8,4096]{1,0:T(8,128)S(1)} %collective-permute-done.7.refs_0_, f32[1,64,4096]{2,1,0:T(8,128)} %shard_map.39.refs_1_), custom_call_target="tpu_custom_call", output_to_operand_aliasing={{}: (1, {})} | custom-call | tf_op jit(solution)/shard_map/pallas_call | solution.py:546
  (3 shorter events, 0.0 us)
Async XLA Ops:
  0.0 3.2 %collective-permute-start = (f32[64,4096]{1,0:T(8,128)}, f32[64,4096]{1,0:T(8,128)S(1)}, u32[]{:S(2)}, u32[]{:S(2)}) collective-permute-start(f32[64,4096]{1,0:T(8,128)} %bitcast.1), channel_id=1, source_target_pairs={{0,4},{1,5},{2,6},{3,7},{4,0},{5,1},{6,2},{7,3},{8,12},{9,13},{10,... | collective-permute-start | bytes 3145736 | tf_op jit(solution)/shard_map/ppermute | solution.py:35
  3.3 6.8 %collective-permute-start.3 = (f32[8,9216]{1,0:T(8,128)S(1)}, f32[8,9216]{1,0:T(8,128)S(1)}, u32[]{:S(2)}, u32[]{:S(2)}) collective-permute-start(f32[8,9216]{1,0:T(8,128)S(1)} %get-tuple-element.46), channel_id=1, source_target_pairs={{0,16},{1,4},{2,5},{3,6},{4,1},{5,2},{6,3},{7,23},{8,24},{9,12},{1... | collective-permute-start | bytes 884744 | tf_op jit(solution)/shard_map/ppermute | solution.py:35
  4.9 6.5 %collective-permute-start.2 = (f32[8,5120]{1,0:T(8,128)S(1)}, f32[8,5120]{1,0:T(8,128)S(1)}, u32[]{:S(2)}, u32[]{:S(2)}) collective-permute-start(f32[8,5120]{1,0:T(8,128)S(1)} %get-tuple-element.40), channel_id=1, source_target_pairs={{0,8},{1,9},{2,10},{3,11},{4,12},{5,13},{6,14},{7,15},{8,0},{9,1},... | collective-permute-start | bytes 491528 | tf_op jit(solution)/shard_map/ppermute | solution.py:35
  7.1 7.7 %collective-permute-start.1 = (f32[8,5120]{1,0:T(8,128)S(1)}, f32[8,5120]{1,0:T(8,128)S(1)}, u32[]{:S(2)}, u32[]{:S(2)}) collective-permute-start(f32[8,5120]{1,0:T(8,128)S(1)} %get-tuple-element.38), channel_id=1, source_target_pairs={{0,8},{1,9},{2,10},{3,11},{4,12},{5,13},{6,14},{7,15},{8,0},{9,1},... | collective-permute-start | bytes 491528 | tf_op jit(solution)/shard_map/ppermute | solution.py:35
  14.8 1.8 %collective-permute-start.4 = (f32[8,2048]{1,0:T(8,128)S(1)}, f32[8,2048]{1,0:T(8,128)S(1)}, u32[]{:S(2)}, u32[]{:S(2)}) collective-permute-start(f32[8,2048]{1,0:T(8,128)S(1)} %shard_map.33), channel_id=1, source_target_pairs={{0,4},{1,5},{2,6},{3,7},{4,0},{5,1},{6,2},{7,3},{8,12},{9,13},{10,... | collective-permute-start | bytes 196616 | tf_op jit(solution)/shard_map/ppermute | solution.py:35
  17.4 10.9 %collective-permute-start.8 = (f32[32,4096]{1,0:T(8,128)S(1)}, f32[32,4096]{1,0:T(8,128)S(1)}, u32[]{:S(2)}, u32[]{:S(2)}) collective-permute-start(f32[32,4096]{1,0:T(8,128)S(1)} %get-tuple-element.62), channel_id=1, source_target_pairs={{0,4},{1,5},{2,6},{3,7},{4,0},{5,1},{6,2},{7,3},{8,12},{9,13},{10,... | collective-permute-start | bytes 1572872 | tf_op jit(solution)/shard_map/ppermute | solution.py:35
  17.8 6.8 %collective-permute-start.5 = (f32[8,4096]{1,0:T(8,128)S(1)}, f32[8,4096]{1,0:T(8,128)S(1)}, u32[]{:S(2)}, u32[]{:S(2)}) collective-permute-start(f32[8,4096]{1,0:T(8,128)S(1)} %get-tuple-element.42), channel_id=1, source_target_pairs={{0,8},{1,9},{2,10},{3,11},{4,12},{5,13},{6,14},{7,15},{16,24},{17,... | collective-permute-start | bytes 393224 | tf_op jit(solution)/shard_map/ppermute | solution.py:35
  19.1 7.7 %collective-permute-start.6 = (f32[8,3072]{1,0:T(8,128)S(1)}, f32[8,3072]{1,0:T(8,128)S(1)}, u32[]{:S(2)}, u32[]{:S(2)}) collective-permute-start(f32[8,3072]{1,0:T(8,128)S(1)} %get-tuple-element.47), channel_id=1, source_target_pairs={{0,8},{1,9},{2,10},{3,11},{4,12},{5,13},{6,14},{7,15},{8,0},{9,1},... | collective-permute-start | bytes 294920 | tf_op jit(solution)/shard_map/ppermute | solution.py:35
  25.1 3.2 %collective-permute-start.9 = (f32[8,4096]{1,0:T(8,128)S(1)}, f32[8,4096]{1,0:T(8,128)S(1)}, u32[]{:S(2)}, u32[]{:S(2)}) collective-permute-start(f32[8,4096]{1,0:T(8,128)S(1)} %get-tuple-element.63), channel_id=1, source_target_pairs={{0,4},{1,5},{2,6},{3,7},{4,0},{5,1},{6,2},{7,3},{8,12},{9,13},{10,... | collective-permute-start | bytes 393224 | tf_op jit(solution)/shard_map/ppermute | solution.py:35
  27.4 1.9 %collective-permute-start.7 = (f32[8,4096]{1,0:T(8,128)S(1)}, f32[8,4096]{1,0:T(8,128)S(1)}, u32[]{:S(2)}, u32[]{:S(2)}) collective-permute-start(f32[8,4096]{1,0:T(8,128)S(1)} %get-tuple-element.55), channel_id=1, source_target_pairs={{0,4},{1,5},{2,6},{3,7},{4,0},{5,1},{6,2},{7,3},{8,12},{9,13},{10,... | collective-permute-start | bytes 393224 | tf_op jit(solution)/shard_map/ppermute | solution.py:35

commit v5 on v4

--- a/solution.py
+++ b/solution.py
@@ -326,12 +326,11 @@
 def outer_kernel(half, own, other, drive, got, sent, ends):
     core, chip = place()
     first = core == 0
-    a, b, d, kept = outer_window(half, own, other, drive, got)
-    f_a, g_a = start_of(a, d, kept)
 
     @pl.when(chip == 0)
     def _():
-        f_b, g_b = start_of(b, d, kept)
+        a, b, d, kept = outer_window(half, own, other, drive, got)
+        (f_a, g_a), (f_b, g_b) = start_of(a, d, kept), start_of(b, d, kept)
         e_a = g_a + (f_a - g_a)
         e_b = kept(coarse_of(e_a, around(e_a), d)) + (f_b - g_b)
         frame = pltpu.roll(e_b, 16 - CUT, 0)[:8]
@@ -339,23 +338,19 @@
         ends[0:16, :] = e_a
         ends[16:32, :] = e_b
 
+
+def outer_state_kernel(half, own, other, drive, got, mine, theirs, state):
+    core, chip = place()
+    first = core == 0
+
     @pl.when(chip > 0)
     def _():
-        ends[0:16, :] = f_a - g_a
-
-
-def outer_state_kernel(half, own, other, drive, got, mine, theirs, ends, state):
-    core, chip = place()
-    first = core == 0
-
-    @pl.when(chip > 0)
-    def _():
-        _, b, d, kept = outer_window(half, own, other, drive, got)
-        f_b, g_b = start_of(b, d, kept)
+        a, b, d, kept = outer_window(half, own, other, drive, got)
+        (f_a, g_a), (f_b, g_b) = start_of(a, d, kept), start_of(b, d, kept)
         rows = pl.ds(pl.multiple_of((half - WIDE) * core, 8), 16)
         before = picked(first, mine[rows, :], theirs[rows, :])
         d_rows = pl.ds(pl.multiple_of((2 * half - 16) * core, 8), 16)
-        fields = zip((ends[0:16, :], f_b - g_b, d), (*before, drive[d_rows, :]))
+        fields = zip((f_a - g_a, f_b - g_b, d), (*before, drive[d_rows, :]))
         for kind, (v, near) in enumerate(fields):
             top = jnp.where(first, v[:8], near[:8])
             mid = jnp.where(first, mixed(v[8:], near[:8]), mixed(near[8:], v[:8]))
@@ -697,7 +692,7 @@
     (state_3,) = compute(
         functools.partial(outer_state_kernel, half),
         [(3 * 24, width)],
-        (own, other, held, got, delta_own, delta_other, ends_3),
+        (own, other, held, got, delta_own, delta_other),
     )
     near_keep, near_send, frame = compute(
         functools.partial(inner_end, half),

time: 30.2 us -> 30.7 us (1.017)
  transfers between devices with their start and end apart: 10 -> 10, of which waited for: 5 -> 4; matrix products, arithmetic and copies ran while one was open for 0% -> 0% of each run, Pallas kernels for 26% -> 26%
where the time goes in v5:
time: 30.7 us; the launch traced here: 30.5 us
  starting transfers between devices  12 us (39%)
  Pallas kernels  9.58 us (31%)
  waiting for transfers between devices  8.74 us (28%)
    ppermute x10, starting transfers between devices, routed(): return lax.ppermute(block, AXES, pairs)  12 us
    ppermute x10, waiting for transfers between devices, routed(): return lax.ppermute(block, AXES, pairs)  8.74 us
    pallas_call x11, Pallas kernels, compute(): pl.pallas_call(kernel, out_shape=shapes, in_specs=[vmem] * len(args), out...  6.34 us
    pallas_call x2, Pallas kernels, written(): pl.pallas_call(functools.partial(write_kernel, half, into is not None), o...  1.69 us
    pallas_call x1, Pallas kernels, two_chips(): pl.pallas_call(functools.partial(load_kernel, half), out_shape=[jax.Shape...  1.55 us
  transfers between devices with their start and end apart: 10, of which 4 were waited for; matrix products, arithmetic and copies ran while one was open for 0% of the time, Pallas kernels for 26%

profile of v5, /device:TPU:3, one launch (start us, length us, event | category | flops | bytes accessed | tf_op | source)
XLA Modules:
  0.0 30.5 jit_solution(2493604251116743045)
XLA Ops:
  0.0 0.7 %collective-permute-start = (f32[64,4096]{1,0:T(8,128)}, f32[64,4096]{1,0:T(8,128)S(1)}, u32[]{:S(2)}, u32[]{:S(2)}) collective-permute-start(f32[64,4096]{1,0:T(8,128)} %bitcast.1), channel_id=1, source_target_pairs={{0,4},{1,5},{2,6},{3,7},{4,0},{5,1},{6,2},{7,3},{8,12},{9,13},{10,... | collective-permute-start | bytes 3145736 | tf_op jit(solution)/shard_map/ppermute | solution.py:35
  0.7 1.5 %load.1 = (f32[64,4096]{1,0:T(8,128)S(1)}, f32[64,4096]{1,0:T(8,128)S(1)}, f32[64,4096]{1,0:T(8,128)S(1)}) custom-call(f32[1,64,4096]{2,1,0:T(8,128)} %starts.1, f32[64,4096]{1,0:T(8,128)} %drive.1), custom_call_target="tpu_custom_call" | custom-call | flops 5898240 | bytes 4194304 | tf_op jit(solution)/shard_map/load/pallas_call | solution.py:644
  2.2 0.9 %collective-permute-done.other = f32[64,4096]{1,0:T(8,128)S(1)} collective-permute-done((f32[64,4096]{1,0:T(8,128)}, f32[64,4096]{1,0:T(8,128)S(1)}, u32[]{:S(2)}, u32[]{:S(2)}) %collective-permute-start) | collective-permute-done | bytes 1048608 | tf_op jit(solution)/shard_map/ppermute | solution.py:35
  3.2 0.1 shard_map.29
  3.3 1.6 %collective-permute-start.3 = (f32[8,9216]{1,0:T(8,128)S(1)}, f32[8,9216]{1,0:T(8,128)S(1)}, u32[]{:S(2)}, u32[]{:S(2)}) collective-permute-start(f32[8,9216]{1,0:T(8,128)S(1)} %get-tuple-element.46), channel_id=1, source_target_pairs={{0,16},{1,4},{2,5},{3,6},{4,1},{5,2},{6,3},{7,23},{8,24},{9,12},{1... | collective-permute-start | bytes 884744 | tf_op jit(solution)/shard_map/ppermute | solution.py:35
  4.9 2.2 %collective-permute-start.2 = (f32[8,5120]{1,0:T(8,128)S(1)}, f32[8,5120]{1,0:T(8,128)S(1)}, u32[]{:S(2)}, u32[]{:S(2)}) collective-permute-start(f32[8,5120]{1,0:T(8,128)S(1)} %get-tuple-element.40), channel_id=1, source_target_pairs={{0,8},{1,9},{2,10},{3,11},{4,12},{5,13},{6,14},{7,15},{8,0},{9,1},... | collective-permute-start | bytes 491528 | tf_op jit(solution)/shard_map/ppermute | solution.py:35
  7.1 0.0 collective-permute-start.1
  7.1 2.9 %shard_map.31 = (f32[40,4096]{1,0:T(8,128)S(1)}, f32[40,4096]{1,0:T(8,128)S(1)}) custom-call(f32[64,4096]{1,0:T(8,128)S(1)} %get-tuple-element.35.own, f32[64,4096]{1,0:T(8,128)S(1)} %collective-permute-done.other, f32[64,4096]{1,0:T(8,128)S(1)} %get-tuple-element.45.drive), custom_call_target="tpu_custom_call" | custom-call | tf_op jit(solution)/shard_map/pallas_call | solution.py:99
  10.0 0.0 collective-permute-done.3.got
  10.1 1.2 %collective-permute-done.2.right = f32[8,5120]{1,0:T(8,128)S(1)} collective-permute-done((f32[8,5120]{1,0:T(8,128)S(1)}, f32[8,5120]{1,0:T(8,128)S(1)}, u32[]{:S(2)}, u32[]{:S(2)}) %collective-permute-start.2) | collective-permute-done | bytes 163872 | tf_op jit(solution)/shard_map/ppermute | solution.py:35
  11.3 3.5 %collective-permute-done.1.left = f32[8,5120]{1,0:T(8,128)S(1)} collective-permute-done((f32[8,5120]{1,0:T(8,128)S(1)}, f32[8,5120]{1,0:T(8,128)S(1)}, u32[]{:S(2)}, u32[]{:S(2)}) %collective-permute-start.1) | collective-permute-done | bytes 163872 | tf_op jit(solution)/shard_map/ppermute | solution.py:35
  14.8 0.9 %collective-permute-start.4 = (f32[8,2048]{1,0:T(8,128)S(1)}, f32[8,2048]{1,0:T(8,128)S(1)}, u32[]{:S(2)}, u32[]{:S(2)}) collective-permute-start(f32[8,2048]{1,0:T(8,128)S(1)} %shard_map.33), channel_id=1, source_target_pairs={{0,4},{1,5},{2,6},{3,7},{4,0},{5,1},{6,2},{7,3},{8,12},{9,13},{10,... | collective-permute-start | bytes 196616 | tf_op jit(solution)/shard_map/ppermute | solution.py:35
  15.8 1.4 %shard_map.34.state = f32[72,4096]{1,0:T(8,128)S(1)} custom-call(f32[64,4096]{1,0:T(8,128)S(1)} %get-tuple-element.35.own, f32[64,4096]{1,0:T(8,128)S(1)} %collective-permute-done.other, f32[64,4096]{1,0:T(8,128)S(1)} %get-tuple-element.45.drive, f32[8,9216]{1,0:T(8,128)S(1)} %collective-permute-done.3.got, f32[40,4096]{1,0:T(8,128)S(1)} %get-tuple-element.49.mine, ...), custom_call_target="tpu_custom_call" | custom-call | tf_op jit(solution)/shard_map/pallas_call | solution.py:99
  17.1 0.0 collective-permute-done.4.beyond
  17.1 0.9 %shard_map.35 = (f32[16,4096]{1,0:T(8,128)S(1)}, f32[16,4096]{1,0:T(8,128)S(1)}, f32[24,4096]{1,0:T(8,128)S(1)}) custom-call(f32[8,5120]{1,0:T(8,128)S(1)} %collective-permute-done.1.left, f32[8,5120]{1,0:T(8,128)S(1)} %collective-permute-done.2.right, f32[8,2048]{1,0:T(8,128)S(1)} %collective-permute-done.4.beyond, f32[64,4096]{1,0:T(8,128)S(1)} %get-tuple-element.45.drive, ...), custom_call_target="tpu_custom_call" | custom-call | tf_op jit(solution)/shard_map/pallas_call | solution.py:99
  18.0 0.1 shard_map.38
  18.1 0.1 collective-permute-start.8
  18.2 1.3 %collective-permute-start.5 = (f32[8,4096]{1,0:T(8,128)S(1)}, f32[8,4096]{1,0:T(8,128)S(1)}, u32[]{:S(2)}, u32[]{:S(2)}) collective-permute-start(f32[8,4096]{1,0:T(8,128)S(1)} %get-tuple-element.42), channel_id=1, source_target_pairs={{0,8},{1,9},{2,10},{3,11},{4,12},{5,13},{6,14},{7,15},{16,24},{17,... | collective-permute-start | bytes 393224 | tf_op jit(solution)/shard_map/ppermute | solution.py:35
  19.5 2.2 %collective-permute-start.6 = (f32[8,3072]{1,0:T(8,128)S(1)}, f32[8,3072]{1,0:T(8,128)S(1)}, u32[]{:S(2)}, u32[]{:S(2)}) collective-permute-start(f32[8,3072]{1,0:T(8,128)S(1)} %get-tuple-element.47), channel_id=1, source_target_pairs={{0,8},{1,9},{2,10},{3,11},{4,12},{5,13},{6,14},{7,15},{8,0},{9,1},... | collective-permute-start | bytes 294920 | tf_op jit(solution)/shard_map/ppermute | solution.py:35
  21.6 3.0 %collective-permute-done.5.middle = f32[8,4096]{1,0:T(8,128)S(1)} collective-permute-done((f32[8,4096]{1,0:T(8,128)S(1)}, f32[8,4096]{1,0:T(8,128)S(1)}, u32[]{:S(2)}, u32[]{:S(2)}) %collective-permute-start.5) | collective-permute-done | bytes 131104 | tf_op jit(solution)/shard_map/ppermute | solution.py:35
  24.6 0.5 %shard_map.36 = (f32[8,4096]{1,0:T(8,128)S(1)}, f32[8,4096]{1,0:T(8,128)S(1)}) custom-call(f32[24,4096]{1,0:T(8,128)S(1)} %get-tuple-element.51.inner, f32[8,4096]{1,0:T(8,128)S(1)} %collective-permute-done.5.middle, f32[64,4096]{1,0:T(8,128)S(1)} %get-tuple-element.45.drive, f32[40,4096]{1,0:T(8,128)S(1)} %get-tuple-element.49.mine, ...), custom_call_target="tpu_custom_call" | custom-call | tf_op jit(solution)/shard_map/pallas_call | solution.py:99
  25.2 2.3 %collective-permute-start.9 = (f32[8,4096]{1,0:T(8,128)S(1)}, f32[8,4096]{1,0:T(8,128)S(1)}, u32[]{:S(2)}, u32[]{:S(2)}) collective-permute-start(f32[8,4096]{1,0:T(8,128)S(1)} %get-tuple-element.63), channel_id=1, source_target_pairs={{0,4},{1,5},{2,6},{3,7},{4,0},{5,1},{6,2},{7,3},{8,12},{9,13},{10,... | collective-permute-start | bytes 393224 | tf_op jit(solution)/shard_map/ppermute | solution.py:35
  27.5 0.0 collective-permute-done.6.outer
  27.5 0.5 %shard_map.37 = (f32[8,4096]{1,0:T(8,128)S(1)}, f32[8,4096]{1,0:T(8,128)S(1)}) custom-call(f32[24,4096]{1,0:T(8,128)S(1)} %get-tuple-element.51.inner, f32[8,4096]{1,0:T(8,128)S(1)} %collective-permute-done.5.middle, f32[8,3072]{1,0:T(8,128)S(1)} %collective-permute-done.6.outer, f32[72,4096]{1,0:T(8,128)S(1)} %shard_map.34.state), custom_call_target="tpu_custom_call" | custom-call | tf_op jit(solution)/shard_map/pallas_call | solution.py:99
  28.0 0.6 %collective-permute-start.7 = (f32[8,4096]{1,0:T(8,128)S(1)}, f32[8,4096]{1,0:T(8,128)S(1)}, u32[]{:S(2)}, u32[]{:S(2)}) collective-permute-start(f32[8,4096]{1,0:T(8,128)S(1)} %get-tuple-element.54), channel_id=1, source_target_pairs={{0,4},{1,5},{2,6},{3,7},{4,0},{5,1},{6,2},{7,3},{8,12},{9,13},{10,... | collective-permute-start | bytes 393224 | tf_op jit(solution)/shard_map/ppermute | solution.py:35
  28.7 0.0 collective-permute-done.9.refs_3_
  28.7 0.0 collective-permute-done.8.refs_1_
  28.7 1.0 %shard_map.39.refs_1_ = f32[1,64,4096]{2,1,0:T(8,128)} custom-call(f32[32,4096]{1,0:T(8,128)S(1)} %get-tuple-element.61.refs_0_, f32[32,4096]{1,0:T(8,128)S(1)} %collective-permute-done.8.refs_1_, f32[8,4096]{1,0:T(8,128)S(1)} %get-tuple-element.52.refs_2_, f32[8,4096]{1,0:T(8,128)S(1)} %collective-permute-done.9.refs_3_, ...), custom_call_target="tpu_custom_call" | custom-call | tf_op jit(solution)/shard_map/pallas_call | solution.py:541
  29.6 0.0 collective-permute-done.7.refs_0_
  29.7 0.7 %shard_map.40 = f32[1,64,4096]{2,1,0:T(8,128)} custom-call(f32[8,4096]{1,0:T(8,128)S(1)} %collective-permute-done.7.refs_0_, f32[1,64,4096]{2,1,0:T(8,128)} %shard_map.39.refs_1_), custom_call_target="tpu_custom_call", output_to_operand_aliasing={{}: (1, {})} | custom-call | tf_op jit(solution)/shard_map/pallas_call | solution.py:541
  (4 shorter events, 0.0 us)
Async XLA Ops:
  0.0 3.2 %collective-permute-start = (f32[64,4096]{1,0:T(8,128)}, f32[64,4096]{1,0:T(8,128)S(1)}, u32[]{:S(2)}, u32[]{:S(2)}) collective-permute-start(f32[64,4096]{1,0:T(8,128)} %bitcast.1), channel_id=1, source_target_pairs={{0,4},{1,5},{2,6},{3,7},{4,0},{5,1},{6,2},{7,3},{8,12},{9,13},{10,... | collective-permute-start | bytes 3145736 | tf_op jit(solution)/shard_map/ppermute | solution.py:35
  3.3 6.8 %collective-permute-start.3 = (f32[8,9216]{1,0:T(8,128)S(1)}, f32[8,9216]{1,0:T(8,128)S(1)}, u32[]{:S(2)}, u32[]{:S(2)}) collective-permute-start(f32[8,9216]{1,0:T(8,128)S(1)} %get-tuple-element.46), channel_id=1, source_target_pairs={{0,16},{1,4},{2,5},{3,6},{4,1},{5,2},{6,3},{7,23},{8,24},{9,12},{1... | collective-permute-start | bytes 884744 | tf_op jit(solution)/shard_map/ppermute | solution.py:35
  4.9 6.5 %collective-permute-start.2 = (f32[8,5120]{1,0:T(8,128)S(1)}, f32[8,5120]{1,0:T(8,128)S(1)}, u32[]{:S(2)}, u32[]{:S(2)}) collective-permute-start(f32[8,5120]{1,0:T(8,128)S(1)} %get-tuple-element.40), channel_id=1, source_target_pairs={{0,8},{1,9},{2,10},{3,11},{4,12},{5,13},{6,14},{7,15},{8,0},{9,1},... | collective-permute-start | bytes 491528 | tf_op jit(solution)/shard_map/ppermute | solution.py:35
  7.1 7.7 %collective-permute-start.1 = (f32[8,5120]{1,0:T(8,128)S(1)}, f32[8,5120]{1,0:T(8,128)S(1)}, u32[]{:S(2)}, u32[]{:S(2)}) collective-permute-start(f32[8,5120]{1,0:T(8,128)S(1)} %get-tuple-element.38), channel_id=1, source_target_pairs={{0,8},{1,9},{2,10},{3,11},{4,12},{5,13},{6,14},{7,15},{8,0},{9,1},... | collective-permute-start | bytes 491528 | tf_op jit(solution)/shard_map/ppermute | solution.py:35
  14.8 2.3 %collective-permute-start.4 = (f32[8,2048]{1,0:T(8,128)S(1)}, f32[8,2048]{1,0:T(8,128)S(1)}, u32[]{:S(2)}, u32[]{:S(2)}) collective-permute-start(f32[8,2048]{1,0:T(8,128)S(1)} %shard_map.33), channel_id=1, source_target_pairs={{0,4},{1,5},{2,6},{3,7},{4,0},{5,1},{6,2},{7,3},{8,12},{9,13},{10,... | collective-permute-start | bytes 196616 | tf_op jit(solution)/shard_map/ppermute | solution.py:35
  18.1 10.6 %collective-permute-start.8 = (f32[32,4096]{1,0:T(8,128)S(1)}, f32[32,4096]{1,0:T(8,128)S(1)}, u32[]{:S(2)}, u32[]{:S(2)}) collective-permute-start(f32[32,4096]{1,0:T(8,128)S(1)} %get-tuple-element.62), channel_id=1, source_target_pairs={{0,4},{1,5},{2,6},{3,7},{4,0},{5,1},{6,2},{7,3},{8,12},{9,13},{10,... | collective-permute-start | bytes 1572872 | tf_op jit(solution)/shard_map/ppermute | solution.py:35
  18.2 6.5 %collective-permute-start.5 = (f32[8,4096]{1,0:T(8,128)S(1)}, f32[8,4096]{1,0:T(8,128)S(1)}, u32[]{:S(2)}, u32[]{:S(2)}) collective-permute-start(f32[8,4096]{1,0:T(8,128)S(1)} %get-tuple-element.42), channel_id=1, source_target_pairs={{0,8},{1,9},{2,10},{3,11},{4,12},{5,13},{6,14},{7,15},{16,24},{17,... | collective-permute-start | bytes 393224 | tf_op jit(solution)/shard_map/ppermute | solution.py:35
  19.5 8.0 %collective-permute-start.6 = (f32[8,3072]{1,0:T(8,128)S(1)}, f32[8,3072]{1,0:T(8,128)S(1)}, u32[]{:S(2)}, u32[]{:S(2)}) collective-permute-start(f32[8,3072]{1,0:T(8,128)S(1)} %get-tuple-element.47), channel_id=1, source_target_pairs={{0,8},{1,9},{2,10},{3,11},{4,12},{5,13},{6,14},{7,15},{8,0},{9,1},... | collective-permute-start | bytes 294920 | tf_op jit(solution)/shard_map/ppermute | solution.py:35
  25.2 3.5 %collective-permute-start.9 = (f32[8,4096]{1,0:T(8,128)S(1)}, f32[8,4096]{1,0:T(8,128)S(1)}, u32[]{:S(2)}, u32[]{:S(2)}) collective-permute-start(f32[8,4096]{1,0:T(8,128)S(1)} %get-tuple-element.63), channel_id=1, source_target_pairs={{0,4},{1,5},{2,6},{3,7},{4,0},{5,1},{6,2},{7,3},{8,12},{9,13},{10,... | collective-permute-start | bytes 393224 | tf_op jit(solution)/shard_map/ppermute | solution.py:35
  28.0 1.6 %collective-permute-start.7 = (f32[8,4096]{1,0:T(8,128)S(1)}, f32[8,4096]{1,0:T(8,128)S(1)}, u32[]{:S(2)}, u32[]{:S(2)}) collective-permute-start(f32[8,4096]{1,0:T(8,128)S(1)} %get-tuple-element.54), channel_id=1, source_target_pairs={{0,4},{1,5},{2,6},{3,7},{4,0},{5,1},{6,2},{7,3},{8,12},{9,13},{10,... | collective-permute-start | bytes 393224 | tf_op jit(solution)/shard_map/ppermute | solution.py:35
